TPU v7x, 512 devices: a whole 4x4x16 slice. The times are simulated.
512 devices in a mesh: ifg: 128 (over x, z, core), tile: 4 (over y).
Axes of the slice: x: 4, y: 4, z: 16, core: 2. Of those that a mesh axis runs over, the one named last changes fastest.
Arguments:
- ifgs: bfloat16 [1152, 8, 16384], P('ifg', 'tile'), may hold values from -12 to 12
- pairs: int32 [1152, 2], replicated, may hold values from 0 to 299, as said below
- pseudo_inverse: bfloat16 [300, 1152], P(None, 'ifg'), may hold values from -0.1875 to 0.1875
- ref_pixels: int32 [64], replicated, may hold values from 0 to 131071
- epochs: int32 [8], replicated, may hold values from 8 to 291
Outputs:
- coefficients: float32 [16, 8, 16384], P(None, 'tile', 'ifg')
- misfit_rms: float32 [8, 16384], P('tile', 'ifg')
Inputs may be any that keep to these rules, and one draw needn't show every extreme that they name: pairs[k, 0] < pairs[k, 1] <= pairs[k, 0] + 6.
All inputs are finite; a program needn't handle non-finite values.
Results may differ from a plain program's by a relative error of at most 0.0029.
Values may be sent and summed in bfloat16 or wider, within the bound.
A program may use at most 64 MiB of HBM per device.

v0:
```python
import math

import jax
import jax.numpy as jnp
from jax import lax
from jax.sharding import PartitionSpec as P

EPS = 1e-06
RIDGE = 1.0


def design(epochs, count):
    index = jnp.arange(count, dtype=jnp.int32)
    days = index.astype(jnp.float32)
    scaled = 2.0 * days / (count - 1) - 1.0
    years = days * 12.0 / 365.25
    smooth = jnp.stack(
        [
            jnp.ones_like(days),
            scaled,
            scaled * scaled,
            scaled * scaled * scaled,
            jnp.sin(2.0 * math.pi * years),
            jnp.cos(2.0 * math.pi * years),
            jnp.sin(4.0 * math.pi * years),
            jnp.cos(4.0 * math.pi * years),
        ],
        axis=1,
    )
    jumps = (index[:, None] >= epochs[None, :]).astype(jnp.float32)
    return jnp.concatenate([smooth, jumps], axis=1)


def fit_operator(epochs, count):
    matrix = design(epochs, count)
    normal = jnp.dot(
        matrix.T, matrix, precision=lax.Precision.HIGHEST, preferred_element_type=jnp.float32
    )
    normal = normal + RIDGE * jnp.eye(matrix.shape[1], dtype=jnp.float32)
    factor = jnp.linalg.cholesky(normal)
    return jax.scipy.linalg.cho_solve((factor, True), matrix.T)


def incidence_matrix(pairs, count):
    dates = jnp.arange(count, dtype=jnp.int32)
    later = (pairs[:, 1:2] == dates[None, :]).astype(jnp.float32)
    earlier = (pairs[:, 0:1] == dates[None, :]).astype(jnp.float32)
    return later - earlier


def shards(ifgs, pairs, pseudo_inverse, ref_pixels, epochs):
    row_count = ifgs.shape[1]
    col_total = ifgs.shape[2]
    col_count = col_total // lax.axis_size("ifg")
    region_size = ref_pixels.shape[0]
    date_count = pseudo_inverse.shape[0]
    tile_index = lax.axis_index("tile")
    ifg_index = lax.axis_index("ifg")
    ref_row = ref_pixels // col_total
    ref_col = ref_pixels % col_total
    row_rel = ref_row - tile_index * row_count
    in_tile = (row_rel >= 0) & (row_rel < row_count)
    row_safe = jnp.clip(row_rel, 0, row_count - 1)
    regrouped = lax.all_to_all(ifgs, "ifg", split_axis=2, concat_axis=0, tiled=True)
    col_rel = ref_col - ifg_index * col_count
    in_block = in_tile & (col_rel >= 0) & (col_rel < col_count)
    col_safe = jnp.clip(col_rel, 0, col_count - 1)
    values = regrouped[:, row_safe, col_safe].astype(jnp.float32)
    partial_value = jnp.sum(jnp.where(in_block[None, :], values, 0.0), axis=1)
    totals = lax.psum(partial_value, ("ifg", "tile"))
    corrected = (regrouped.astype(jnp.float32) - (totals / region_size)[:, None, None]).astype(
        jnp.bfloat16
    )
    pixel_rows = corrected.reshape(corrected.shape[0], row_count * col_count)
    displacement = jnp.dot(
        lax.all_gather(pseudo_inverse, "ifg", axis=1, tiled=True),
        pixel_rows,
        preferred_element_type=jnp.float32,
    )
    operator = fit_operator(epochs, date_count)
    coeffs = jnp.dot(
        operator, displacement, precision=lax.Precision.HIGHEST, preferred_element_type=jnp.float32
    )
    incidence = incidence_matrix(pairs, date_count)
    predicted = jnp.dot(
        incidence, displacement, precision=lax.Precision.HIGHEST, preferred_element_type=jnp.float32
    )
    misfit = pixel_rows.astype(jnp.float32) - predicted
    spread = jnp.sqrt(jnp.mean(misfit * misfit, axis=0) + EPS)
    return (
        coeffs.reshape(operator.shape[0], row_count, col_count),
        spread.reshape(row_count, col_count),
    )


def solution(mesh):
    in_specs = (P("ifg", "tile", None), P(), P(None, "ifg"), P(), P())
    out_specs = (P(None, "tile", "ifg"), P("tile", "ifg"))
    return jax.shard_map(shards, mesh=mesh, in_specs=in_specs, out_specs=out_specs, check_vma=False)
```

profile of v0, /device:TPU:1, one launch (start us, length us, event | category | flops | bytes accessed | tf_op | source)
XLA Modules:
  0.0 324.9 jit_solution(13141437848219759013)
XLA Ops:
  0.6 15.8 %copy.18 = bf16[9,2,16384]{0,1,2:T(2,128)(2,1)} copy(bf16[9,2,16384]{2,1,0:T(2,128)(2,1)} %param.5) | data formatting | bytes 1179648 | tf_op args[0]
  16.4 18.2 %reshape.101 = bf16[128,2,1152]{2,1,0:T(2,128)(2,1)} reshape(bf16[16384,2,9]{2,1,0:T(2,128)(2,1)} %bitcast.43) | data formatting | bytes 1179648
  34.7 20.5 %all-to-all-start = ((bf16[128,2,1152]{2,1,0:T(2,128)(2,1)}), bf16[128,2,1152]{2,1,0:T(2,128)(2,1)S(1)}, u32[]{:S(2)}, u32[]{:S(2)}) async-start(bf16[128,2,1152]{2,1,0:T(2,128)(2,1)} %reshape.101), calls=%async_computation | async-start | bytes 1179648 | tf_op jit(solution)/shard_map/all_to_all | solution.py:64
  55.6 0.2 fusion.35
  55.8 1.5 cholesky.17
  57.3 0.6 compare_reduce_fusion
  57.9 0.6 fusion.11
  58.6 1.2 custom-call.10
  59.8 118.4 %all-gather = bf16[128,9,300]{2,1,0:T(8,128)(2,1)S(1)} all-gather(bf16[1,9,300]{2,1,0:T(8,128)(2,1)S(1)} %bitcast.47), channel_id=1, replica_groups=mesh['ifg'=128,'tile'=4] {'ifg'}, dimensions={0}, use_global_device_ids=true | all-gather | bytes 696600 | tf_op jit(solution)/shard_map/all_gather | solution.py:76
  178.2 0.7 reshape.98
  179.0 0.2 fusion.14
  179.2 0.2 fusion.12
  179.4 19.3 %reshape.102 = bf16[16384,2,9]{2,1,0:T(2,128)(2,1)} reshape(bf16[128,2,1152]{2,1,0:T(2,128)(2,1)S(1)} %all-to-all-done) | data formatting | bytes 1179648
  198.7 16.6 %copy.19 = bf16[9,2,128,128]{3,1,0,2:T(2,128)(2,1)S(1)} copy(bf16[9,2,128,128]{0,1,3,2:T(2,128)(2,1)} %bitcast.42) | data formatting | bytes 1179648 | tf_op jit(solution)/shard_map/all_to_all | solution.py:64
  215.2 0.4 bitcast_convert_fusion
  215.7 0.6 copy.20
  216.3 1.2 gather_fusion
  217.5 0.1 select_reduce_fusion
  217.6 102.6 %psum.7 = f32[1152]{0:T(1024)S(1)} all-reduce(f32[1152]{0:T(1024)S(1)} %select_reduce_fusion), channel_id=1, replica_groups=mesh['ifg'=128,'tile'=4] {'ifg','tile'}, use_global_device_ids=true, to_apply=%region_3.4 | all-reduce | flops 1152 | bytes 9216 | tf_op jit(solution)/shard_map/psum | solution.py:70
  320.1 0.7 fusion.31
  320.8 0.2 fusion.36
  321.0 0.7 reshape.77
  321.7 2.6 fusion.4
  324.4 0.6 sqrt_bitcast_fusion
  (23 shorter events, 0.6 us)
Async XLA Ops:
  34.7 20.8 %copy-start.2 = (s32[8]{0:T(128)S(1)}, s32[8]{0:T(128)}, u32[]{:S(2)}) copy-start(s32[8]{0:T(128)} %param.9) | copy-start | bytes 100
  34.7 25.2 %copy-start = (bf16[300,9]{0,1:T(8,128)(2,1)S(1)}, bf16[300,9]{0,1:T(8,128)(2,1)}, u32[]{:S(2)}) copy-start(bf16[300,9]{0,1:T(8,128)(2,1)} %param.7) | copy-start | bytes 16204
  34.7 144.7 %all-to-all-start = ((bf16[128,2,1152]{2,1,0:T(2,128)(2,1)}), bf16[128,2,1152]{2,1,0:T(2,128)(2,1)S(1)}, u32[]{:S(2)}, u32[]{:S(2)}) async-start(bf16[128,2,1152]{2,1,0:T(2,128)(2,1)} %reshape.101), calls=%async_computation | async-start | bytes 1179648 | tf_op jit(solution)/shard_map/all_to_all | solution.py:64
  178.2 0.7 copy-start.1
  178.2 0.7 copy-start.3
where the time goes:
time: 327 us; the launch traced here: 325 us
  blocking collectives  221 us (68%)
  local copies, waits for them, and re-layouts  73.1 us (22%)
  starting transfers between devices  20.5 us (6%)
  other arithmetic  5.45 us (2%)
  matrix products  4.07 us (1%)
    all_gather x1, blocking collectives, shards(): lax.all_gather(pseudo_inverse, 'ifg', axis=1, tiled=True)  118 us
    psum x1, blocking collectives, shards(): totals = lax.psum(partial_value, ('ifg', 'tile'))  103 us
    unnamed x12, local copies, waits for them, and re-layouts  54 us
    all_to_all x1, starting transfers between devices, shards(): lax.all_to_all(ifgs, 'ifg', split_axis=2, concat_axis=0, tiled=True)  20.5 us
    all_to_all x2, local copies, waits for them, and re-layouts, shards(): lax.all_to_all(ifgs, 'ifg', split_axis=2, concat_axis=0, tiled=True)  17.2 us
  transfers between devices with their start and end apart: 1, of which 0 were waited for; matrix products, arithmetic and copies ran while one was open for 2% of the time, Pallas kernels for 0%

commit v1 on v0

v1 whole, which is shorter than its diff:
```python
import functools
import math

import jax
import jax.numpy as jnp
from jax import lax
from jax.experimental import pallas as pl
from jax.experimental.pallas import tpu as pltpu
from jax.sharding import PartitionSpec as P

EPS = 1e-06
RIDGE = 1.0


def design(epochs, count):
    index = jnp.arange(count, dtype=jnp.int32)
    days = index.astype(jnp.float32)
    scaled = 2.0 * days / (count - 1) - 1.0
    years = days * 12.0 / 365.25
    smooth = jnp.stack(
        [
            jnp.ones_like(days),
            scaled,
            scaled * scaled,
            scaled * scaled * scaled,
            jnp.sin(2.0 * math.pi * years),
            jnp.cos(2.0 * math.pi * years),
            jnp.sin(4.0 * math.pi * years),
            jnp.cos(4.0 * math.pi * years),
        ],
        axis=1,
    )
    jumps = (index[:, None] >= epochs[None, :]).astype(jnp.float32)
    return jnp.concatenate([smooth, jumps], axis=1)


def fit_operator(epochs, count):
    matrix = design(epochs, count)
    normal = jnp.dot(
        matrix.T, matrix, precision=lax.Precision.HIGHEST, preferred_element_type=jnp.float32
    )
    normal = normal + RIDGE * jnp.eye(matrix.shape[1], dtype=jnp.float32)
    factor = jnp.linalg.cholesky(normal)
    return jax.scipy.linalg.cho_solve((factor, True), matrix.T)


def incidence_matrix(pairs, count):
    dates = jnp.arange(count, dtype=jnp.int32)
    later = (pairs[:, 1:2] == dates[None, :]).astype(jnp.float32)
    earlier = (pairs[:, 0:1] == dates[None, :]).astype(jnp.float32)
    return later - earlier


MESH = pl.DeviceIdType.MESH
LANES = 128


def reference_sums(region, ifgs, out):
    count, rows, width = ifgs.shape
    lane = lax.broadcasted_iota(jnp.int32, out.shape, 2)
    row = lax.broadcasted_iota(jnp.int32, out.shape, 1) + lax.axis_index("tile") * rows

    def collect(i, total):
        pixel = region[i]
        col = lax.rem(pixel, width)
        block = lax.div(col, LANES) * LANES
        values = ifgs[:, :, pl.ds(pl.multiple_of(block, LANES), LANES)].astype(jnp.float32)
        hit = (lane == lax.rem(col, LANES)) & (row == lax.div(pixel, width))
        return total + jnp.where(hit, values, 0.0)

    out[...] = lax.fori_loop(0, region.shape[0], collect, jnp.zeros(out.shape, jnp.float32))


def exchange(dims, ifgs, inverse, local, moved, gathered, sent, sums, sem):
    nx, nz, nc, tiles, region_size = dims
    group = nx * nz * nc
    half = nz // 2
    tile = lax.axis_index("tile")
    me = lax.axis_index("ifg")
    my_c = lax.rem(me, nc)
    my_z = lax.rem(lax.div(me, nc), nz)
    my_x = lax.div(me, nc * nz)

    def place(step):
        plane = lax.div(step, nx * nc)
        inner = lax.rem(step, nx * nc)
        j = lax.div(plane + 1, 2)
        odd = lax.rem(plane, 2)
        dz = odd * (half - j) + (1 - odd) * (half + j)
        dx = nx - 1 - lax.div(inner, nc)
        dc = nc - 1 - lax.rem(inner, nc)
        return lax.rem(my_x + dx, nx), lax.rem(my_z + dz, nz), lax.rem(my_c + dc, nc)

    def device(x, z, c):
        return {"ifg": (x * nz + z) * nc + c, "tile": tile}

    barrier = pltpu.get_barrier_semaphore()

    def greet(step, carry):
        pl.semaphore_signal(
            barrier, inc=1, device_id=device(*place(step)), device_id_type=MESH
        )
        return carry

    lax.fori_loop(0, group - 1, greet, 0)
    for d in range(1, tiles):
        pl.semaphore_signal(
            barrier,
            inc=1,
            device_id={"ifg": me, "tile": lax.rem(tile + d, tiles)},
            device_id_type=MESH,
        )

    own = pltpu.make_async_copy(inverse, gathered.at[my_c, my_x, my_z], sem.at[0])
    own.start()

    count, rows, _ = ifgs.shape
    pl.semaphore_wait(barrier, group - 1 + tiles - 1)

    def partial_copy(d):
        return pltpu.make_async_remote_copy(
            src_ref=local,
            dst_ref=sums.at[d - 1],
            send_sem=sem.at[d],
            recv_sem=sem.at[tiles + d],
            device_id={"ifg": me, "tile": lax.rem(tile + d, tiles)},
            device_id_type=MESH,
        )

    for d in range(1, tiles):
        partial_copy(d).start()

    base = 2 * tiles

    def z_copy(dz, ref):
        return pltpu.make_async_remote_copy(
            src_ref=ref,
            dst_ref=gathered.at[my_c, my_x, my_z],
            send_sem=sem.at[base],
            recv_sem=sem.at[base + 1],
            device_id=device(my_x, lax.rem(my_z + dz, nz), my_c),
            device_id_type=MESH,
        )

    def send_z(i, carry):
        j = lax.div(i + 1, 2)
        odd = lax.rem(i, 2)
        z_copy(odd * (half - j) + (1 - odd) * (half + j), inverse).start()
        return carry

    lax.fori_loop(0, nz - 1, send_z, 0)

    for d in range(1, tiles):
        partial_copy(d).wait()
    total = local[...]
    for d in range(1, tiles):
        total = total + sums[d - 1]
    mean = jnp.sum(total, axis=(1, 2), keepdims=True) / region_size
    mean = jnp.broadcast_to(mean, (count, rows, LANES))

    def corrected(x, z, c):
        col = ((x * nz + z) * nc + c) * LANES
        values = ifgs[:, :, pl.ds(pl.multiple_of(col, LANES), LANES)].astype(jnp.float32)
        return (values - mean).astype(jnp.bfloat16)

    def prepare(step, carry):
        sent[step] = corrected(*place(step))
        return carry

    def block_copy(step):
        return pltpu.make_async_remote_copy(
            src_ref=sent.at[step],
            dst_ref=moved.at[my_c, my_x, my_z],
            send_sem=sem.at[base + 2],
            recv_sem=sem.at[base + 3],
            device_id=device(*place(step)),
            device_id_type=MESH,
        )

    def send_block(step, carry):
        block_copy(step).start()
        return carry

    plane = nx * nc
    first = plane * 5
    lax.fori_loop(0, plane, prepare, 0)

    def both(step, carry):
        send_block(step, carry)
        return prepare(step + plane, carry)

    lax.fori_loop(0, first, both, 0)

    own.wait()
    arrived = pltpu.make_async_remote_copy(
        src_ref=gathered.at[0, 0, pl.ds(0, nz - 1)],
        dst_ref=gathered.at[0, 0, pl.ds(0, nz - 1)],
        send_sem=sem.at[base],
        recv_sem=sem.at[base + 1],
        device_id=device(my_x, lax.rem(my_z + 1, nz), my_c),
        device_id_type=MESH,
    )
    arrived.wait()

    def x_copy(d):
        return pltpu.make_async_remote_copy(
            src_ref=gathered.at[my_c, my_x],
            dst_ref=gathered.at[my_c, my_x],
            send_sem=sem.at[base + 3 + 2 * d],
            recv_sem=sem.at[base + 4 + 2 * d],
            device_id=device(lax.rem(my_x + d, nx), my_z, my_c),
            device_id_type=MESH,
        )

    for d in range(1, nx):
        x_copy(d).start()

    lax.fori_loop(first, group - 1 - plane, both, 0)
    lax.fori_loop(group - 1 - plane, group - 1, send_block, 0)
    moved[my_c, my_x, my_z] = corrected(my_x, my_z, my_c)

    for d in range(1, nx):
        x_copy(d).wait()
    core = pltpu.make_async_remote_copy(
        src_ref=gathered.at[my_c],
        dst_ref=gathered.at[my_c],
        send_sem=sem.at[base + 5 + 2 * nx],
        recv_sem=sem.at[base + 6 + 2 * nx],
        device_id=device(my_x, my_z, lax.rem(my_c + 1, nc)),
        device_id_type=MESH,
    )
    core.start()
    everything = pltpu.make_async_remote_copy(
        src_ref=sent.at[pl.ds(0, group - 1)],
        dst_ref=sent.at[pl.ds(0, group - 1)],
        send_sem=sem.at[base + 2],
        recv_sem=sem.at[base + 3],
        device_id=device(my_x, lax.rem(my_z + 1, nz), my_c),
        device_id_type=MESH,
    )
    everything.wait()
    core.wait()


def shards(ifgs, pairs, pseudo_inverse, ref_pixels, epochs, physical):
    nx, nz, nc = physical
    count, row_count, _ = ifgs.shape
    group = lax.axis_size("ifg")
    tiles = lax.axis_size("tile")
    date_count = pseudo_inverse.shape[0]
    padded = -(-date_count // LANES) * LANES
    pairs_up = -(-count // 2)
    inverse = jnp.pad(
        pseudo_inverse.T, ((0, 2 * pairs_up - count), (0, padded - date_count))
    ).reshape(pairs_up, 2, padded)
    vmem = pl.BlockSpec(memory_space=pltpu.VMEM)
    local = pl.pallas_call(
        reference_sums,
        out_shape=jax.ShapeDtypeStruct((count, row_count, LANES), jnp.float32),
        in_specs=[pl.BlockSpec(memory_space=pltpu.SMEM), vmem],
        out_specs=vmem,
    )(ref_pixels, ifgs)
    moved, gathered = pl.pallas_call(
        functools.partial(exchange, (nx, nz, nc, tiles, ref_pixels.shape[0])),
        out_shape=(
            jax.ShapeDtypeStruct((nc, nx, nz, count, row_count, LANES), jnp.bfloat16),
            jax.ShapeDtypeStruct((nc, nx, nz, pairs_up, 2, padded), jnp.bfloat16),
        ),
        in_specs=[vmem, vmem, vmem],
        out_specs=(vmem, vmem),
        scratch_shapes=[
            pltpu.VMEM((group, count, row_count, LANES), jnp.bfloat16),
            pltpu.VMEM((tiles - 1, count, row_count, LANES), jnp.float32),
            pltpu.SemaphoreType.DMA((2 * tiles + 7 + 2 * nx,)),
        ],
        compiler_params=pltpu.CompilerParams(collective_id=0, has_side_effects=True),
    )(ifgs, inverse, local)
    total = group * count
    pixel_rows = moved.reshape(total, row_count * LANES)
    operator = gathered.reshape(group, 2 * pairs_up, padded)[:, :count, :date_count]
    displacement = lax.dot_general(
        operator.reshape(total, date_count),
        pixel_rows,
        (((0,), (0,)), ((), ())),
        preferred_element_type=jnp.float32,
    )
    fit = fit_operator(epochs, date_count)
    coeffs = jnp.dot(
        fit, displacement, precision=lax.Precision.HIGHEST, preferred_element_type=jnp.float32
    )
    ordered = pairs.reshape(nx, nz, nc, count, 2).transpose(2, 0, 1, 3, 4).reshape(total, 2)
    incidence = incidence_matrix(ordered, date_count)
    predicted = jnp.dot(
        incidence, displacement, precision=lax.Precision.HIGHEST, preferred_element_type=jnp.float32
    )
    misfit = pixel_rows.astype(jnp.float32) - predicted
    spread = jnp.sqrt(jnp.mean(misfit * misfit, axis=0) + EPS)
    return (
        coeffs.reshape(fit.shape[0], row_count, LANES),
        spread.reshape(row_count, LANES),
    )


def solution(mesh):
    nx, nc = 4, 2
    nz = mesh.shape["ifg"] // (nx * nc)
    in_specs = (P("ifg", "tile", None), P(), P(None, "ifg"), P(), P())
    out_specs = (P(None, "tile", "ifg"), P("tile", "ifg"))
    run = functools.partial(shards, physical=(nx, nz, nc))
    return jax.shard_map(run, mesh=mesh, in_specs=in_specs, out_specs=out_specs, check_vma=False)
```

time: 327 us -> 72.5 us (0.22)
  blocking collectives: 221 us -> 0 us
  local copies, waits for them, and re-layouts: 73.1 us -> 5.69 us
  Pallas kernels: 0 us -> 56.3 us
  starting transfers between devices: 20.5 us -> 0 us
    all_gather x1 -> x0, blocking collectives: 118 us -> none  [shards(): lax.all_gather(pseudo_inverse, 'ifg', axis=1, tiled=True)]
    psum x1 -> x0, blocking collectives: 103 us -> none  [shards(): totals = lax.psum(partial_value, ('ifg', 'tile'))]
    pallas_call x0 -> x2, Pallas kernels: none -> 56.3 us  [the longest x1 53.5 us: shards(): pl.pallas_call(functools.partial(exchange, (nx, nz, nc, tiles, ref_pixels...]
    unnamed x12 -> x4, local copies, waits for them, and re-layouts: 54 us -> 0.4 us
    all_to_all x1 -> x0, starting transfers between devices: 20.5 us -> none  [shards(): lax.all_to_all(ifgs, 'ifg', split_axis=2, concat_axis=0, tiled=True)]
    all_to_all x2 -> x0, local copies, waits for them, and re-layouts: 17.2 us -> none  [shards(): lax.all_to_all(ifgs, 'ifg', split_axis=2, concat_axis=0, tiled=True)]
  transfers between devices with their start and end apart: 1 -> 0, of which waited for: 0 -> 0; matrix products, arithmetic and copies ran while one was open for 2% -> 0% of each run, Pallas kernels for 0% -> 0%
where the time goes in v1:
time: 72.5 us; the launch traced here: 72.2 us
  Pallas kernels  56.3 us (78%)
  local copies, waits for them, and re-layouts  5.69 us (8%)
  other arithmetic  5.55 us (8%)
  matrix products  3.8 us (5%)
  between operations  0.77 us (1%)
    pallas_call x1, Pallas kernels, shards(): pl.pallas_call(functools.partial(exchange, (nx, nz, nc, tiles, ref_pixels...  53.5 us
    pallas_call x1, Pallas kernels, shards(): pl.pallas_call(reference_sums, out_shape=jax.ShapeDtypeStruct((count, row...  2.82 us
    dot_general x1, matrix products, shards(): jnp.dot(incidence, displacement, precision=lax.Precision.HIGHEST, preferr...  2.59 us
    another operation x3, other arithmetic, fit_operator(): factor = jnp.linalg.cholesky(normal)  2.13 us
    another operation x2, other arithmetic, fit_operator(): return jax.scipy.linalg.cho_solve((factor, True), matrix.T)  1.88 us

profile of v1, /device:TPU:1, one launch (start us, length us, event | category | flops | bytes accessed | tf_op | source)
XLA Modules:
  0.0 72.2 jit_solution(982827219741440371)
XLA Ops:
  0.6 0.1 fusion.21
  0.9 0.7 %fusion.12 = f32[300,8]{0,1:T(8,128)S(1)} fusion(s32[8]{0:T(128)} %param.9), kind=kLoop, calls=%fused_computation.14 | loop fusion | flops 4800 | bytes 9632 | tf_op jit(solution)/shard_map/convert_element_type | solution.py:33
  1.6 0.2 fusion.26
  1.9 1.5 %cholesky.17 = f32[16,16]{1,0:T(8,128)S(1)} custom-call(f32[16,16]{1,0:T(8,128)S(1)} %fusion.19), custom_call_target="Cholesky" | custom-call | tf_op jit(solution)/shard_map/jit(cholesky)/cholesky | solution.py:43
  3.4 0.6 compare_reduce_fusion
  4.0 0.6 fusion.13
  4.7 1.2 %custom-call.10 = f32[1,16,16]{1,2,0:T(8,128)S(1)} custom-call(f32[1,16,16]{2,1,0:T(8,128)S(1)} %fusion.13), custom_call_target="InvertDiagBlocksLowerTriangular" | custom-call | tf_op jit(solution)/shard_map/jit(_cho_solve)/triangular_solve | solution.py:44
  5.9 0.2 fusion.16
  6.1 0.2 fusion.14
  6.3 0.7 pad.4
  7.0 0.6 reshape.89.inverse
  7.6 2.8 %shard_map.68.local = f32[9,2,128]{2,1,0:T(2,128)} custom-call(s32[64]{0:T(128)} %region.1, bf16[9,2,16384]{2,1,0:T(2,128)(2,1)} %ifgs.3), custom_call_target="tpu_custom_call" | custom-call | tf_op jit(solution)/shard_map/pallas_call | solution.py:257
  10.5 53.5 %shard_map.69 = (bf16[2,4,16,9,2,128]{5,4,3,2,1,0:T(2,128)(2,1)}, bf16[2,4,16,5,2,384]{5,4,3,2,1,0:T(2,128)(2,1)}) custom-call(bf16[9,2,16384]{2,1,0:T(2,128)(2,1)} %ifgs.3, bf16[5,2,384]{2,1,0:T(2,128)(2,1)} %reshape.89.inverse, f32[9,2,128]{2,1,0:T(2,128)} %shard_map.68.local), custom_call_target="tpu_custom_call" | custom-call | tf_op jit(solution)/shard_map/pallas_call | solution.py:263
  64.0 1.4 %copy.13 = bf16[2,4,16,5,2,384]{5,2,1,0,4,3:T(8,128)(2,1)S(1)} copy(bf16[2,4,16,5,2,384]{5,4,3,2,1,0:T(2,128)(2,1)} %get-tuple-element.4) | data formatting | bytes 1966080 | tf_op jit(solution)/shard_map/pallas_call | solution.py:263
  65.5 0.6 copy.14
  66.1 0.7 reshape.91
  66.7 0.4 copy-done.1
  67.1 0.4 fusion.9
  67.6 0.2 fusion.27
  67.8 0.7 reshape.93
  68.5 0.3 reshape.94
  68.7 0.2 reshape.95
  69.0 2.6 %fusion.4 = f32[256]{0:T(256)S(1)} fusion(f32[300,256]{1,0:T(8,128)S(1)} %fusion.9, s32[1152]{0:T(1024)S(1)} %get-tuple-element.7, s32[1152]{0:T(1024)S(1)} %get-tuple-element.6, bf16[144,8,2,128]{3,2,1,0:T(2,128)(2,1)S(1)} %bitcast.42), kind=kOutput, calls=%fused_computation.7 | convolution fusion | flops 1064590592 | bytes 907264 | tf_op jit(solution)/shard_map/dot_general | solution.py:293
  71.6 0.6 sqrt_bitcast_fusion
  (14 shorter events, 0.4 us)
Async XLA Ops:
  66.0 1.1 %copy-start.1 = (bf16[2,4,16,9,2,128]{5,4,3,2,1,0:T(2,128)(2,1)S(1)}, bf16[2,4,16,9,2,128]{5,4,3,2,1,0:T(2,128)(2,1)}, u32[]{:S(2)}) copy-start(bf16[2,4,16,9,2,128]{5,4,3,2,1,0:T(2,128)(2,1)} %get-tuple-element.5) | copy-start | bytes 1769476
  67.1 1.3 %copy-start = (s32[1152,2]{0,1:T(2,128)S(1)}, s32[1152,2]{0,1:T(2,128)}, u32[]{:S(2)}) copy-start(s32[1152,2]{0,1:T(2,128)} %param.6) | copy-start | bytes 27652

commit v2 on v1

v2 whole, which is shorter than its diff:
```python
import functools

import jax
import jax.numpy as jnp
import numpy as np
from jax import lax
from jax.experimental import pallas as pl
from jax.experimental.pallas import tpu as pltpu
from jax.sharding import PartitionSpec as P

EPS = 1e-06
RIDGE = 1.0


def smooth_columns(count, padded):
    days = np.arange(count, dtype=np.float64)
    scaled = 2.0 * days / (count - 1) - 1.0
    years = days * 12.0 / 365.25
    smooth = np.stack(
        [
            np.ones_like(days),
            scaled,
            scaled**2,
            scaled**3,
            np.sin(2.0 * np.pi * years),
            np.cos(2.0 * np.pi * years),
            np.sin(4.0 * np.pi * years),
            np.cos(4.0 * np.pi * years),
        ]
    )
    return np.pad(smooth, ((0, 0), (0, padded - count))).astype(np.float32)


def fit_operator(smooth, epochs, count):
    steps = epochs.shape[0]
    index = lax.broadcasted_iota(jnp.int32, (steps, smooth.shape[1]), 1)
    which = lax.broadcasted_iota(jnp.int32, (steps, smooth.shape[1]), 0)
    start = jnp.zeros_like(index)
    for e in range(steps):
        start = jnp.where(which == e, epochs[e], start)
    jumps = jnp.where((index >= start) & (index < count), 1.0, 0.0)
    right = jnp.concatenate([smooth, jumps], axis=0)
    terms = right.shape[0]
    normal = lax.dot_general(
        right,
        right,
        (((1,), (1,)), ((), ())),
        precision=lax.Precision.HIGHEST,
        preferred_element_type=jnp.float32,
    )
    line = lax.broadcasted_iota(jnp.int32, (terms, terms), 0)
    left = normal + jnp.where(
        line == lax.broadcasted_iota(jnp.int32, (terms, terms), 1), RIDGE, 0.0
    )
    wide = lax.broadcasted_iota(jnp.int32, right.shape, 0)
    for j in range(terms):
        pivot = left[j : j + 1, j : j + 1]
        left_row = left[j : j + 1, :] / pivot
        right_row = right[j : j + 1, :] / pivot
        factor = left[:, j : j + 1]
        left = jnp.where(line == j, left_row, left - factor * left_row)
        right = jnp.where(wide == j, right_row, right - factor * right_row)
    return right


def incidence_matrix(pairs, count):
    dates = jnp.arange(count, dtype=jnp.int32)
    later = (pairs[:, 1:2] == dates[None, :]).astype(jnp.float32)
    earlier = (pairs[:, 0:1] == dates[None, :]).astype(jnp.float32)
    return later - earlier


MESH = pl.DeviceIdType.MESH
LANES = 128


def reference_counts(region, tile, rows, width):
    blocks = width // LANES
    line = lax.shift_right_arithmetic(region, width.bit_length() - 1) - tile * rows
    col = lax.bitwise_and(region, width - 1)
    block = lax.shift_right_arithmetic(col, LANES.bit_length() - 1)
    lane = lax.bitwise_and(col, LANES - 1)
    key = jnp.where((line >= 0) & (line < rows), block * rows + line, -1)
    listed = region.shape[1]
    spots = lax.broadcasted_iota(jnp.int32, (blocks * rows, listed), 0) == key
    lanes = lax.broadcasted_iota(jnp.int32, (LANES, listed), 0) == lane
    return lax.dot_general(
        jnp.where(spots, 1.0, 0.0),
        jnp.where(lanes, 1.0, 0.0),
        (((1,), (1,)), ((), ())),
        preferred_element_type=jnp.float32,
    )


def exchange(
    dims, epochs, ifgs, inverse, region, smooth,
    moved, gathered, fit,
    sent, piece, counts, local, sums, sem,
):
    nx, nz, nc, tiles = dims
    group = nx * nz * nc
    half = nz // 2
    tile = lax.axis_index("tile")
    me = lax.axis_index("ifg")
    my_c = lax.rem(me, nc)
    my_z = lax.rem(lax.div(me, nc), nz)
    my_x = lax.div(me, nc * nz)

    def place(step):
        plane = lax.div(step, nx * nc)
        inner = lax.rem(step, nx * nc)
        j = lax.div(plane + 1, 2)
        odd = lax.rem(plane, 2)
        dz = odd * (half - j) + (1 - odd) * (half + j)
        dx = nx - 1 - lax.div(inner, nc)
        dc = nc - 1 - lax.rem(inner, nc)
        return lax.rem(my_x + dx, nx), lax.rem(my_z + dz, nz), lax.rem(my_c + dc, nc)

    def device(x, z, c):
        return {"ifg": (x * nz + z) * nc + c, "tile": tile}

    barrier = pltpu.get_barrier_semaphore()

    def greet(step, carry):
        pl.semaphore_signal(
            barrier, inc=1, device_id=device(*place(step)), device_id_type=MESH
        )
        return carry

    lax.fori_loop(0, group - 1, greet, 0)
    for d in range(1, tiles):
        pl.semaphore_signal(
            barrier,
            inc=1,
            device_id={"ifg": me, "tile": lax.rem(tile + d, tiles)},
            device_id_type=MESH,
        )

    count, rows, width = ifgs.shape
    dates = inverse.shape[1]
    piece[...] = jnp.zeros_like(piece)
    last = -(-dates // LANES) - 1
    for q in range(last + 1):
        lo, hi = q * LANES, min(q * LANES + LANES, dates)

        @pl.when(tile == q if q < last else tile >= last)
        def _(lo=lo, hi=hi):
            for k in range(count):
                piece[k // 2, k % 2 : k % 2 + 1, : hi - lo] = inverse[k : k + 1, lo:hi]

    own = pltpu.make_async_copy(piece, gathered.at[my_c, tile, my_x, my_z], sem.at[0])
    own.start()

    counts[...] = reference_counts(region[...], tile, rows, width)

    def collect(block, total):
        col = pl.multiple_of(block * LANES, LANES)
        values = ifgs[:, :, pl.ds(col, LANES)].astype(jnp.float32)
        return total + values * counts[pl.ds(block * rows, rows), :][None]

    local[...] = lax.fori_loop(
        0, width // LANES, collect, jnp.zeros((count, rows, LANES), jnp.float32)
    )
    pl.semaphore_wait(barrier, group - 1 + tiles - 1)

    def partial_copy(d):
        return pltpu.make_async_remote_copy(
            src_ref=local,
            dst_ref=sums.at[d - 1],
            send_sem=sem.at[d],
            recv_sem=sem.at[tiles + d],
            device_id={"ifg": me, "tile": lax.rem(tile + d, tiles)},
            device_id_type=MESH,
        )

    for d in range(1, tiles):
        partial_copy(d).start()

    base = 2 * tiles

    def z_copy(dz, ref):
        return pltpu.make_async_remote_copy(
            src_ref=ref,
            dst_ref=gathered.at[my_c, tile, my_x, my_z],
            send_sem=sem.at[base],
            recv_sem=sem.at[base + 1],
            device_id=device(my_x, lax.rem(my_z + dz, nz), my_c),
            device_id_type=MESH,
        )

    def send_z(i, carry):
        j = lax.div(i + 1, 2)
        odd = lax.rem(i, 2)
        z_copy(odd * (half - j) + (1 - odd) * (half + j), piece).start()
        return carry

    lax.fori_loop(0, nz - 1, send_z, 0)
    fit[...] = fit_operator(smooth[...], epochs, dates)

    for d in range(1, tiles):
        partial_copy(d).wait()
    total = local[...]
    for d in range(1, tiles):
        total = total + sums[d - 1]
    mean = jnp.sum(total, axis=(1, 2), keepdims=True) / region.shape[1]
    mean = jnp.broadcast_to(mean, (count, rows, LANES))

    def corrected(x, z, c):
        col = ((x * nz + z) * nc + c) * LANES
        values = ifgs[:, :, pl.ds(pl.multiple_of(col, LANES), LANES)].astype(jnp.float32)
        return (values - mean).astype(jnp.bfloat16)

    def prepare(step, carry):
        sent[step] = corrected(*place(step))
        return carry

    def block_copy(step):
        return pltpu.make_async_remote_copy(
            src_ref=sent.at[step],
            dst_ref=moved.at[my_c, my_x, my_z],
            send_sem=sem.at[base + 2],
            recv_sem=sem.at[base + 3],
            device_id=device(*place(step)),
            device_id_type=MESH,
        )

    def send_block(step, carry):
        block_copy(step).start()
        return carry

    plane = nx * nc
    first = plane * 5
    lax.fori_loop(0, plane, prepare, 0)

    def both(step, carry):
        send_block(step, carry)
        return prepare(step + plane, carry)

    lax.fori_loop(0, first, both, 0)

    own.wait()
    arrived = pltpu.make_async_remote_copy(
        src_ref=gathered.at[0, 0, 0, pl.ds(0, nz - 1)],
        dst_ref=gathered.at[0, 0, 0, pl.ds(0, nz - 1)],
        send_sem=sem.at[base],
        recv_sem=sem.at[base + 1],
        device_id=device(my_x, lax.rem(my_z + 1, nz), my_c),
        device_id_type=MESH,
    )
    arrived.wait()

    def x_copy(d):
        return pltpu.make_async_remote_copy(
            src_ref=gathered.at[my_c, tile, my_x],
            dst_ref=gathered.at[my_c, tile, my_x],
            send_sem=sem.at[base + 2 + 2 * d],
            recv_sem=sem.at[base + 3 + 2 * d],
            device_id=device(lax.rem(my_x + d, nx), my_z, my_c),
            device_id_type=MESH,
        )

    for d in range(1, nx):
        x_copy(d).start()

    lax.fori_loop(first, group - 1 - plane, both, 0)
    lax.fori_loop(group - 1 - plane, group - 1, send_block, 0)
    moved[my_c, my_x, my_z] = corrected(my_x, my_z, my_c)

    for d in range(1, nx):
        x_copy(d).wait()

    over = base + 2 + 2 * nx

    def tile_copy(d):
        return pltpu.make_async_remote_copy(
            src_ref=gathered.at[my_c, tile],
            dst_ref=gathered.at[my_c, tile],
            send_sem=sem.at[over + 2 * d],
            recv_sem=sem.at[over + 1 + 2 * d],
            device_id={"ifg": me, "tile": lax.rem(tile + d, tiles)},
            device_id_type=MESH,
        )

    for d in range(1, tiles):
        tile_copy(d).start()
    for d in range(1, tiles):
        tile_copy(d).wait()
    core = pltpu.make_async_remote_copy(
        src_ref=gathered.at[my_c],
        dst_ref=gathered.at[my_c],
        send_sem=sem.at[over],
        recv_sem=sem.at[over + 1],
        device_id=device(my_x, my_z, lax.rem(my_c + 1, nc)),
        device_id_type=MESH,
    )
    core.start()
    everything = pltpu.make_async_remote_copy(
        src_ref=sent.at[pl.ds(0, group - 1)],
        dst_ref=sent.at[pl.ds(0, group - 1)],
        send_sem=sem.at[base + 2],
        recv_sem=sem.at[base + 3],
        device_id=device(my_x, lax.rem(my_z + 1, nz), my_c),
        device_id_type=MESH,
    )
    everything.wait()
    core.wait()


def shards(ifgs, pairs, pseudo_inverse, ref_pixels, epochs, physical):
    nx, nz, nc = physical
    count, row_count, col_total = ifgs.shape
    group = lax.axis_size("ifg")
    tiles = lax.axis_size("tile")
    date_count = pseudo_inverse.shape[0]
    padded = -(-date_count // LANES) * LANES
    pairs_up = -(-count // 2)
    vmem = pl.BlockSpec(memory_space=pltpu.VMEM)
    smooth = jnp.asarray(smooth_columns(date_count, padded))
    terms = smooth.shape[0] + epochs.shape[0]
    moved, gathered, fit = pl.pallas_call(
        functools.partial(exchange, (nx, nz, nc, tiles)),
        out_shape=(
            jax.ShapeDtypeStruct((nc, nx, nz, count, row_count, LANES), jnp.bfloat16),
            jax.ShapeDtypeStruct((nc, tiles, nx, nz, pairs_up, 2, LANES), jnp.bfloat16),
            jax.ShapeDtypeStruct((terms, padded), jnp.float32),
        ),
        in_specs=[pl.BlockSpec(memory_space=pltpu.SMEM)] + [vmem] * 4,
        out_specs=(vmem,) * 3,
        scratch_shapes=[
            pltpu.VMEM((group, count, row_count, LANES), jnp.bfloat16),
            pltpu.VMEM((pairs_up, 2, LANES), jnp.bfloat16),
            pltpu.VMEM((col_total // LANES * row_count, LANES), jnp.float32),
            pltpu.VMEM((count, row_count, LANES), jnp.float32),
            pltpu.VMEM((tiles - 1, count, row_count, LANES), jnp.float32),
            pltpu.SemaphoreType.DMA((4 * tiles + 2 * nx + 4,)),
        ],
        compiler_params=pltpu.CompilerParams(collective_id=0, has_side_effects=True),
    )(epochs, ifgs, pseudo_inverse.T, ref_pixels[None, :], smooth)
    total = group * count
    pixel_rows = moved.reshape(total, row_count * LANES)
    operator = gathered[:, : padded // LANES].transpose(0, 2, 3, 4, 5, 1, 6)
    operator = operator.reshape(group, 2 * pairs_up, padded)[:, :count, :date_count]
    displacement = lax.dot_general(
        operator.reshape(total, date_count),
        pixel_rows,
        (((0,), (0,)), ((), ())),
        preferred_element_type=jnp.float32,
    )
    fit = fit[:, :date_count]
    coeffs = jnp.dot(
        fit, displacement, precision=lax.Precision.HIGHEST, preferred_element_type=jnp.float32
    )
    ordered = pairs.reshape(nx, nz, nc, count, 2).transpose(2, 0, 1, 3, 4).reshape(total, 2)
    incidence = incidence_matrix(ordered, date_count)
    predicted = jnp.dot(
        incidence, displacement, precision=lax.Precision.HIGHEST, preferred_element_type=jnp.float32
    )
    misfit = pixel_rows.astype(jnp.float32) - predicted
    spread = jnp.sqrt(jnp.mean(misfit * misfit, axis=0) + EPS)
    return (
        coeffs.reshape(terms, row_count, LANES),
        spread.reshape(row_count, LANES),
    )


def solution(mesh):
    nx, nc = 4, 2
    nz = mesh.shape["ifg"] // (nx * nc)
    in_specs = (P("ifg", "tile", None), P(), P(None, "ifg"), P(), P())
    out_specs = (P(None, "tile", "ifg"), P("tile", "ifg"))
    run = functools.partial(shards, physical=(nx, nz, nc))
    return jax.shard_map(run, mesh=mesh, in_specs=in_specs, out_specs=out_specs, check_vma=False)
```

time: 72.5 us -> 65.2 us (0.90)
  other arithmetic: 5.55 us -> 0.57 us
  Pallas kernels: 56.3 us -> 53.6 us
  local copies, waits for them, and re-layouts: 5.69 us -> 6.77 us
    another operation x5 -> x0, other arithmetic: 4.01 us -> none  [the longest x3 2.13 us: fit_operator(): factor = jnp.linalg.cholesky(normal)]
    transpose x0 -> x2, local copies, waits for them, and re-layouts: none -> 2.76 us  [shards(): operator = gathered[:, :padded // LANES].transpose(0, 2, 3, 4, 5, 1, 6)]
    pallas_call x2 -> x1, Pallas kernels: 56.3 us -> 53.6 us  [shards(): pl.pallas_call(functools.partial(exchange, (nx, nz, nc, tiles)), out_shap...]
    pallas_call x1 -> x0, local copies, waits for them, and re-layouts: 1.36 us -> none  [shards(): pl.pallas_call(functools.partial(exchange, (nx, nz, nc, tiles, ref_pixels...]
    convert_element_type x1 -> x0, other arithmetic: 0.73 us -> none  [design(): jumps = (index[:, None] >= epochs[None, :]).astype(jnp.float32)]
where the time goes in v2:
time: 65.2 us; the launch traced here: 65 us
  Pallas kernels  53.6 us (82%)
  local copies, waits for them, and re-layouts  6.77 us (10%)
  matrix products  3.23 us (5%)
  between operations  0.75 us (1%)
    pallas_call x1, Pallas kernels, shards(): pl.pallas_call(functools.partial(exchange, (nx, nz, nc, tiles)), out_shap...  53.6 us
    transpose x2, local copies, waits for them, and re-layouts, shards(): operator = gathered[:, :padded // LANES].transpose(0, 2, 3, 4, 5, 1, 6)  2.76 us
    dot_general x1, matrix products, shards(): jnp.dot(incidence, displacement, precision=lax.Precision.HIGHEST, preferr...  2.58 us

profile of v2, /device:TPU:1, one launch (start us, length us, event | category | flops | bytes accessed | tf_op | source)
XLA Modules:
  0.0 65.0 jit_solution(15258619241791698158)
XLA Ops:
  0.6 53.6 %shard_map.77 = (bf16[2,4,16,9,2,128]{5,4,3,2,1,0:T(2,128)(2,1)}, bf16[2,4,4,16,5,2,128]{6,5,4,3,2,1,0:T(2,128)(2,1)}, f32[16,384]{1,0:T(8,128)}) custom-call(s32[8]{0:T(128)} %epochs.1, bf16[9,2,16384]{2,1,0:T(2,128)(2,1)} %ifgs.1, bf16[9,300]{1,0:T(8,128)(2,1)} %bitcast.25, s32[1,64]{1,0:T(1,128)} %bitcast.26, f32[8,384]{1,0:T(8,128)} %constant.9.clone.smooth), custom_call_target="tpu_custom_call" | custom-call | tf_op jit(solution)/shard_map/pallas_call | solution.py:320
  54.3 1.9 %slice_bitcast_fusion = bf16[2,4,16,5,2,3,128]{6,4,3,2,1,5,0:T(2,128)(2,1)S(1)} fusion(bf16[2,4,4,16,5,2,128]{6,5,4,3,2,1,0:T(2,128)(2,1)} %get-tuple-element.6), kind=kLoop, calls=%fused_computation.8 | loop fusion | bytes 1966080 | tf_op jit(solution)/shard_map/transpose | solution.py:341
  56.2 0.8 %copy.8 = bf16[2,4,16,5,2,3,128]{6,5,2,1,0,4,3:T(4,128)(2,1)S(1)} copy(bf16[2,4,16,5,2,3,128]{6,4,3,2,1,5,0:T(2,128)(2,1)S(1)} %slice_bitcast_fusion) | data formatting | bytes 1966080 | tf_op jit(solution)/shard_map/transpose | solution.py:341
  57.1 0.9 %reshape.29 = bf16[128,10,384]{2,0,1:T(8,128)(2,1)S(1)} reshape(bf16[2,4,16,5,2,3,128]{6,5,2,1,0,4,3:T(4,128)(2,1)S(1)} %copy.8) | data formatting | bytes 1966080 | tf_op jit(solution)/shard_map/reshape | solution.py:342
  57.9 0.1 slice.20
  58.0 0.6 copy.9
  58.6 0.0 copy-start.2
  58.6 0.7 %reshape.30 = bf16[1152,300]{1,0:T(8,128)(2,1)S(1)} reshape(bf16[128,9,300]{2,1,0:T(8,128)(2,1)S(1)} %copy.9) | data formatting | bytes 1382400 | tf_op jit(solution)/shard_map/reshape | solution.py:344
  59.3 0.4 copy-done.2
  59.7 0.0 copy-start.1
  59.7 0.4 fusion.9
  60.1 0.3 copy-done.1
  60.4 0.3 reshape.33
  60.7 0.2 reshape.34
  60.9 0.0 copy-start
  60.9 2.6 %fusion.4 = f32[256]{0:T(256)S(1)} fusion(f32[300,256]{1,0:T(8,128)S(1)} %fusion.9, s32[1152]{0:T(1024)S(1)} %get-tuple-element.9, s32[1152]{0:T(1024)S(1)} %get-tuple-element.8, bf16[144,8,2,128]{3,2,1,0:T(2,128)(2,1)S(1)} %bitcast.28), kind=kOutput, calls=%fused_computation.7 | convolution fusion | flops 1064590592 | bytes 907264 | tf_op jit(solution)/shard_map/dot_general | solution.py:355
  63.5 0.6 sqrt_bitcast_fusion
  64.1 0.0 copy-done
  64.1 0.2 fusion.12
  64.3 0.7 %reshape.32 = f32[16,2,128]{2,1,0:T(2,128)} reshape(f32[16,256]{1,0:T(8,128)S(1)} %fusion.12) | data formatting | bytes 32768 | tf_op jit(solution)/shard_map/reshape | solution.py:361
  (2 shorter events, 0.0 us)
Async XLA Ops:
  58.6 1.1 %copy-start.2 = (bf16[2,4,16,9,2,128]{5,4,3,2,1,0:T(2,128)(2,1)S(1)}, bf16[2,4,16,9,2,128]{5,4,3,2,1,0:T(2,128)(2,1)}, u32[]{:S(2)}) copy-start(bf16[2,4,16,9,2,128]{5,4,3,2,1,0:T(2,128)(2,1)} %get-tuple-element.7) | copy-start | bytes 1769476
  59.7 0.7 %copy-start.1 = (s32[1152,2]{0,1:T(2,128)S(1)}, s32[1152,2]{0,1:T(2,128)}, u32[]{:S(2)}) copy-start(s32[1152,2]{0,1:T(2,128)} %param.7) | copy-start | bytes 27652
  60.9 3.2 %copy-start = (f32[16,384]{1,0:T(8,128)S(1)}, f32[16,384]{1,0:T(8,128)}, u32[]{:S(2)}) copy-start(f32[16,384]{1,0:T(8,128)} %get-tuple-element.5) | copy-start | bytes 73732

commit v3 on v2

--- a/solution.py
+++ b/solution.py
@@ -95,7 +95,7 @@
 def exchange(
     dims, epochs, ifgs, inverse, region, smooth,
     moved, gathered, fit,
-    sent, piece, counts, local, sums, sem,
+    sent, piece, column, counts, local, sums, sem,
 ):
     nx, nz, nc, tiles = dims
     group = nx * nz * nc
@@ -119,6 +119,7 @@
     def device(x, z, c):
         return {"ifg": (x * nz + z) * nc + c, "tile": tile}
 
+    column[...] = jnp.zeros_like(column)
     barrier = pltpu.get_barrier_semaphore()
 
     def greet(step, carry):
@@ -145,11 +146,9 @@
 
         @pl.when(tile == q if q < last else tile >= last)
         def _(lo=lo, hi=hi):
-            for k in range(count):
-                piece[k // 2, k % 2 : k % 2 + 1, : hi - lo] = inverse[k : k + 1, lo:hi]
-
-    own = pltpu.make_async_copy(piece, gathered.at[my_c, tile, my_x, my_z], sem.at[0])
-    own.start()
+            piece[:count, : hi - lo] = inverse[:, lo:hi]
+
+    column[my_z] = piece[...]
 
     counts[...] = reference_counts(region[...], tile, rows, width)
 
@@ -177,11 +176,12 @@
         partial_copy(d).start()
 
     base = 2 * tiles
+    even = -(-count // 2) * 2
 
     def z_copy(dz, ref):
         return pltpu.make_async_remote_copy(
             src_ref=ref,
-            dst_ref=gathered.at[my_c, tile, my_x, my_z],
+            dst_ref=column.at[my_z, pl.ds(0, even)],
             send_sem=sem.at[base],
             recv_sem=sem.at[base + 1],
             device_id=device(my_x, lax.rem(my_z + dz, nz), my_c),
@@ -191,7 +191,7 @@
     def send_z(i, carry):
         j = lax.div(i + 1, 2)
         odd = lax.rem(i, 2)
-        z_copy(odd * (half - j) + (1 - odd) * (half + j), piece).start()
+        z_copy(odd * (half - j) + (1 - odd) * (half + j), piece.at[pl.ds(0, even)]).start()
         return carry
 
     lax.fori_loop(0, nz - 1, send_z, 0)
@@ -238,16 +238,28 @@
 
     lax.fori_loop(0, first, both, 0)
 
-    own.wait()
     arrived = pltpu.make_async_remote_copy(
-        src_ref=gathered.at[0, 0, 0, pl.ds(0, nz - 1)],
-        dst_ref=gathered.at[0, 0, 0, pl.ds(0, nz - 1)],
+        src_ref=column.at[pl.ds(0, nz - 1), pl.ds(0, even)],
+        dst_ref=column.at[pl.ds(0, nz - 1), pl.ds(0, even)],
         send_sem=sem.at[base],
         recv_sem=sem.at[base + 1],
         device_id=device(my_x, lax.rem(my_z + 1, nz), my_c),
         device_id_type=MESH,
     )
     arrived.wait()
+    tall = column.shape[1]
+    target = lax.broadcasted_iota(jnp.int32, (nz * count, nz * tall), 0)
+    source = lax.broadcasted_iota(jnp.int32, (nz * count, nz * tall), 1)
+    line = lax.bitwise_and(source, tall - 1)
+    block = lax.shift_right_arithmetic(source, tall.bit_length() - 1)
+    pick = jnp.where((line < count) & (block * count + line == target), 1.0, 0.0)
+    gathered[my_c, tile, my_x] = jnp.dot(
+        pick.astype(jnp.bfloat16),
+        column[...].reshape(nz * tall, LANES),
+        preferred_element_type=jnp.float32,
+    ).astype(jnp.bfloat16)
+    second = first + 2 * plane
+    lax.fori_loop(first, second, both, 0)
 
     def x_copy(d):
         return pltpu.make_async_remote_copy(
@@ -262,7 +274,7 @@
     for d in range(1, nx):
         x_copy(d).start()
 
-    lax.fori_loop(first, group - 1 - plane, both, 0)
+    lax.fori_loop(second, group - 1 - plane, both, 0)
     lax.fori_loop(group - 1 - plane, group - 1, send_block, 0)
     moved[my_c, my_x, my_z] = corrected(my_x, my_z, my_c)
 
@@ -313,7 +325,7 @@
     tiles = lax.axis_size("tile")
     date_count = pseudo_inverse.shape[0]
     padded = -(-date_count // LANES) * LANES
-    pairs_up = -(-count // 2)
+    tall = 16
     vmem = pl.BlockSpec(memory_space=pltpu.VMEM)
     smooth = jnp.asarray(smooth_columns(date_count, padded))
     terms = smooth.shape[0] + epochs.shape[0]
@@ -321,14 +333,15 @@
         functools.partial(exchange, (nx, nz, nc, tiles)),
         out_shape=(
             jax.ShapeDtypeStruct((nc, nx, nz, count, row_count, LANES), jnp.bfloat16),
-            jax.ShapeDtypeStruct((nc, tiles, nx, nz, pairs_up, 2, LANES), jnp.bfloat16),
+            jax.ShapeDtypeStruct((nc, tiles, nx, nz * count, LANES), jnp.bfloat16),
             jax.ShapeDtypeStruct((terms, padded), jnp.float32),
         ),
         in_specs=[pl.BlockSpec(memory_space=pltpu.SMEM)] + [vmem] * 4,
         out_specs=(vmem,) * 3,
         scratch_shapes=[
             pltpu.VMEM((group, count, row_count, LANES), jnp.bfloat16),
-            pltpu.VMEM((pairs_up, 2, LANES), jnp.bfloat16),
+            pltpu.VMEM((tall, LANES), jnp.bfloat16),
+            pltpu.VMEM((nz, tall, LANES), jnp.bfloat16),
             pltpu.VMEM((col_total // LANES * row_count, LANES), jnp.float32),
             pltpu.VMEM((count, row_count, LANES), jnp.float32),
             pltpu.VMEM((tiles - 1, count, row_count, LANES), jnp.float32),
@@ -338,22 +351,20 @@
     )(epochs, ifgs, pseudo_inverse.T, ref_pixels[None, :], smooth)
     total = group * count
     pixel_rows = moved.reshape(total, row_count * LANES)
-    operator = gathered[:, : padded // LANES].transpose(0, 2, 3, 4, 5, 1, 6)
-    operator = operator.reshape(group, 2 * pairs_up, padded)[:, :count, :date_count]
+    operator = gathered[:, : padded // LANES].transpose(0, 2, 3, 1, 4).reshape(total, padded)
     displacement = lax.dot_general(
-        operator.reshape(total, date_count),
+        operator,
         pixel_rows,
         (((0,), (0,)), ((), ())),
         preferred_element_type=jnp.float32,
     )
-    fit = fit[:, :date_count]
     coeffs = jnp.dot(
         fit, displacement, precision=lax.Precision.HIGHEST, preferred_element_type=jnp.float32
     )
     ordered = pairs.reshape(nx, nz, nc, count, 2).transpose(2, 0, 1, 3, 4).reshape(total, 2)
-    incidence = incidence_matrix(ordered, date_count)
+    incidence = incidence_matrix(ordered, padded)
     predicted = jnp.dot(
-        incidence, displacement, precision=lax.Precision.HIGHEST, preferred_element_type=jnp.float32
+        incidence, displacement, precision=lax.Precision.HIGH, preferred_element_type=jnp.float32
     )
     misfit = pixel_rows.astype(jnp.float32) - predicted
     spread = jnp.sqrt(jnp.mean(misfit * misfit, axis=0) + EPS)

time: 65.2 us -> 61.3 us (0.940)
  local copies, waits for them, and re-layouts: 6.77 us -> 3.65 us
  matrix products: 3.23 us -> 2.54 us
    reshape x2 -> x0, local copies, waits for them, and re-layouts: 1.53 us -> none  [the longest x1 0.87 us: shards(): operator.reshape(group, 2 * pairs_up, padded)[:, :count, :date_count]]
    dot_general x2, matrix products: 3.02 us -> 2.24 us  [the longest x1 1.79 us: shards(): jnp.dot(incidence, displacement, precision=lax.Precision.HIGH, preferred_...]
    transpose x2, local copies, waits for them, and re-layouts: 2.76 us -> 1.99 us  [shards(): gathered[:, :padded // LANES].transpose(0, 2, 3, 1, 4)]
    slice x2 -> x0, local copies, waits for them, and re-layouts: 0.67 us -> none  [shards(): operator.reshape(group, 2 * pairs_up, padded)[:, :count, :date_count]]
where the time goes in v3:
time: 61.3 us; the launch traced here: 61.1 us
  Pallas kernels  53.6 us (87%)
  local copies, waits for them, and re-layouts  3.65 us (6%)
  matrix products  2.54 us (4%)
  between operations  0.71 us (1%)
    pallas_call x1, Pallas kernels, shards(): pl.pallas_call(functools.partial(exchange, (nx, nz, nc, tiles)), out_shap...  53.6 us
    transpose x2, local copies, waits for them, and re-layouts, shards(): gathered[:, :padded // LANES].transpose(0, 2, 3, 1, 4)  1.99 us
    dot_general x1, matrix products, shards(): jnp.dot(incidence, displacement, precision=lax.Precision.HIGH, preferred_...  1.79 us

profile of v3, /device:TPU:1, one launch (start us, length us, event | category | flops | bytes accessed | tf_op | source)
XLA Modules:
  0.0 61.1 jit_solution(14732148314898708121)
XLA Ops:
  0.6 53.6 %shard_map.77 = (bf16[2,4,16,9,2,128]{5,4,3,2,1,0:T(2,128)(2,1)}, bf16[2,4,4,144,128]{4,3,2,1,0:T(8,128)(2,1)}, f32[16,384]{1,0:T(8,128)}) custom-call(s32[8]{0:T(128)} %epochs.1, bf16[9,2,16384]{2,1,0:T(2,128)(2,1)} %ifgs.1, bf16[9,300]{1,0:T(8,128)(2,1)} %bitcast.29, s32[1,64]{1,0:T(1,128)} %bitcast.30, f32[8,384]{1,0:T(8,128)} %constant.9.clone.smooth), custom_call_target="tpu_custom_call" | custom-call | tf_op jit(solution)/shard_map/pallas_call | solution.py:332
  54.2 1.2 %slice_bitcast_fusion = bf16[2,4,144,3,128]{4,2,1,3,0:T(8,128)(2,1)S(1)} fusion(bf16[2,4,4,144,128]{4,3,2,1,0:T(8,128)(2,1)} %get-tuple-element.6), kind=kLoop, calls=%fused_computation.13 | loop fusion | bytes 1769472 | tf_op jit(solution)/shard_map/transpose | solution.py:354
  55.5 0.0 copy-start.2
  55.5 0.8 %copy.8 = bf16[2,4,144,3,128]{4,3,2,1,0:T(4,128)(2,1)S(1)} copy(bf16[2,4,144,3,128]{4,2,1,3,0:T(8,128)(2,1)S(1)} %slice_bitcast_fusion) | data formatting | bytes 1769472 | tf_op jit(solution)/shard_map/transpose | solution.py:354
  56.2 0.3 copy-done.2
  56.5 0.0 copy-start.1
  56.5 0.5 fusion.7
  57.0 0.2 copy-done.1
  57.2 0.3 reshape.29
  57.5 0.2 reshape.30
  57.8 0.0 copy-start
  57.8 1.8 %fusion.4 = f32[256]{0:T(256)S(1)} fusion(f32[384,256]{1,0:T(8,128)S(1)} %fusion.7, s32[1152]{0:T(1024)S(1)} %get-tuple-element.9, s32[1152]{0:T(1024)S(1)} %get-tuple-element.8, bf16[144,8,2,128]{3,2,1,0:T(2,128)(2,1)S(1)} %bitcast.32), kind=kOutput, calls=%fused_computation.7 | convolution fusion | flops 682868480 | bytes 993280 | tf_op jit(solution)/shard_map/dot_general | solution.py:366
  59.6 0.6 sqrt_bitcast_fusion
  60.1 0.0 copy-done
  60.1 0.3 fusion.14
  60.4 0.6 %reshape.28 = f32[16,2,128]{2,1,0:T(2,128)} reshape(f32[16,256]{1,0:T(8,128)S(1)} %fusion.14) | data formatting | bytes 32768 | tf_op jit(solution)/shard_map/reshape | solution.py:372
  (2 shorter events, 0.0 us)
Async XLA Ops:
  55.5 1.1 %copy-start.2 = (bf16[2,4,16,9,2,128]{5,4,3,2,1,0:T(2,128)(2,1)S(1)}, bf16[2,4,16,9,2,128]{5,4,3,2,1,0:T(2,128)(2,1)}, u32[]{:S(2)}) copy-start(bf16[2,4,16,9,2,128]{5,4,3,2,1,0:T(2,128)(2,1)} %get-tuple-element.7) | copy-start | bytes 1769476
  56.5 0.7 %copy-start.1 = (s32[1152,2]{0,1:T(2,128)S(1)}, s32[1152,2]{0,1:T(2,128)}, u32[]{:S(2)}) copy-start(s32[1152,2]{0,1:T(2,128)} %param.7) | copy-start | bytes 27652
  57.8 2.4 %copy-start = (f32[16,384]{1,0:T(8,128)S(1)}, f32[16,384]{1,0:T(8,128)}, u32[]{:S(2)}) copy-start(f32[16,384]{1,0:T(8,128)} %get-tuple-element.5) | copy-start | bytes 73732

commit v4 on v3

--- a/solution.py
+++ b/solution.py
@@ -95,7 +95,7 @@
 def exchange(
     dims, epochs, ifgs, inverse, region, smooth,
     moved, gathered, fit,
-    sent, piece, column, counts, local, sums, sem,
+    sent, relayed, piece, column, counts, local, sums, sem,
 ):
     nx, nz, nc, tiles = dims
     group = nx * nz * nc
@@ -195,7 +195,6 @@
         return carry
 
     lax.fori_loop(0, nz - 1, send_z, 0)
-    fit[...] = fit_operator(smooth[...], epochs, dates)
 
     for d in range(1, tiles):
         partial_copy(d).wait()
@@ -230,13 +229,46 @@
 
     plane = nx * nc
     first = plane * 5
+    hops = plane // 2
+    last_sem = sem.shape[0] - 2
+
+    def relay_copy(slot, ref):
+        return pltpu.make_async_remote_copy(
+            src_ref=ref,
+            dst_ref=slot,
+            send_sem=sem.at[last_sem],
+            recv_sem=sem.at[last_sem + 1],
+            device_id=device(my_x, lax.rem(my_z + nz - 1, nz), my_c),
+            device_id_type=MESH,
+        )
+
+    def pass_on(step, carry):
+        x, z, c = place(step)
+        pltpu.make_async_remote_copy(
+            src_ref=relayed.at[step],
+            dst_ref=moved.at[my_c, my_x, lax.rem(my_z + 1, nz)],
+            send_sem=sem.at[base + 2],
+            recv_sem=sem.at[base + 3],
+            device_id=device(x, lax.rem(z + 1, nz), c),
+            device_id_type=MESH,
+        ).start()
+        return carry
+
     lax.fori_loop(0, plane, prepare, 0)
 
     def both(step, carry):
         send_block(step, carry)
         return prepare(step + plane, carry)
 
-    lax.fori_loop(0, first, both, 0)
+    def both_relayed(step, carry):
+        relay_copy(relayed.at[step], sent.at[step]).start()
+        return prepare(step + plane, carry)
+
+    lax.fori_loop(0, hops, both_relayed, 0)
+    lax.fori_loop(hops, 3 * plane, both, 0)
+    relay_copy(relayed, relayed).wait()
+    lax.fori_loop(0, hops, pass_on, 0)
+    lax.fori_loop(3 * plane, first, both, 0)
 
     arrived = pltpu.make_async_remote_copy(
         src_ref=column.at[pl.ds(0, nz - 1), pl.ds(0, even)],
@@ -276,6 +308,7 @@
 
     lax.fori_loop(second, group - 1 - plane, both, 0)
     lax.fori_loop(group - 1 - plane, group - 1, send_block, 0)
+    fit[...] = fit_operator(smooth[...], epochs, dates)
     moved[my_c, my_x, my_z] = corrected(my_x, my_z, my_c)
 
     for d in range(1, nx):
@@ -340,12 +373,13 @@
         out_specs=(vmem,) * 3,
         scratch_shapes=[
             pltpu.VMEM((group, count, row_count, LANES), jnp.bfloat16),
+            pltpu.VMEM((nx * nc // 2, count, row_count, LANES), jnp.bfloat16),
             pltpu.VMEM((tall, LANES), jnp.bfloat16),
             pltpu.VMEM((nz, tall, LANES), jnp.bfloat16),
             pltpu.VMEM((col_total // LANES * row_count, LANES), jnp.float32),
             pltpu.VMEM((count, row_count, LANES), jnp.float32),
             pltpu.VMEM((tiles - 1, count, row_count, LANES), jnp.float32),
-            pltpu.SemaphoreType.DMA((4 * tiles + 2 * nx + 4,)),
+            pltpu.SemaphoreType.DMA((4 * tiles + 2 * nx + 6,)),
         ],
         compiler_params=pltpu.CompilerParams(collective_id=0, has_side_effects=True),
     )(epochs, ifgs, pseudo_inverse.T, ref_pixels[None, :], smooth)

time: 61.3 us -> 62.8 us (1.024)
  Pallas kernels: 53.6 us -> 55 us
    pallas_call x1, Pallas kernels: 53.6 us -> 55 us  [shards(): pl.pallas_call(functools.partial(exchange, (nx, nz, nc, tiles)), out_shap...]
where the time goes in v4:
time: 62.8 us; the launch traced here: 62.5 us
  Pallas kernels  55 us (88%)
  local copies, waits for them, and re-layouts  3.65 us (6%)
  matrix products  2.54 us (4%)
  between operations  0.71 us (1%)
    pallas_call x1, Pallas kernels, shards(): pl.pallas_call(functools.partial(exchange, (nx, nz, nc, tiles)), out_shap...  55 us
    transpose x2, local copies, waits for them, and re-layouts, shards(): gathered[:, :padded // LANES].transpose(0, 2, 3, 1, 4)  1.99 us
    dot_general x1, matrix products, shards(): jnp.dot(incidence, displacement, precision=lax.Precision.HIGH, preferred_...  1.79 us

profile of v4, /device:TPU:1, one launch (start us, length us, event | category | flops | bytes accessed | tf_op | source)
XLA Modules:
  0.0 62.5 jit_solution(16513487390906197187)
XLA Ops:
  0.6 55.0 %shard_map.77 = (bf16[2,4,16,9,2,128]{5,4,3,2,1,0:T(2,128)(2,1)}, bf16[2,4,4,144,128]{4,3,2,1,0:T(8,128)(2,1)}, f32[16,384]{1,0:T(8,128)}) custom-call(s32[8]{0:T(128)} %epochs.1, bf16[9,2,16384]{2,1,0:T(2,128)(2,1)} %ifgs.1, bf16[9,300]{1,0:T(8,128)(2,1)} %bitcast.29, s32[1,64]{1,0:T(1,128)} %bitcast.30, f32[8,384]{1,0:T(8,128)} %constant.9.clone.smooth), custom_call_target="tpu_custom_call" | custom-call | tf_op jit(solution)/shard_map/pallas_call | solution.py:365
  55.7 1.2 %slice_bitcast_fusion = bf16[2,4,144,3,128]{4,2,1,3,0:T(8,128)(2,1)S(1)} fusion(bf16[2,4,4,144,128]{4,3,2,1,0:T(8,128)(2,1)} %get-tuple-element.6), kind=kLoop, calls=%fused_computation.13 | loop fusion | bytes 1769472 | tf_op jit(solution)/shard_map/transpose | solution.py:388
  56.9 0.0 copy-start.2
  56.9 0.8 %copy.8 = bf16[2,4,144,3,128]{4,3,2,1,0:T(4,128)(2,1)S(1)} copy(bf16[2,4,144,3,128]{4,2,1,3,0:T(8,128)(2,1)S(1)} %slice_bitcast_fusion) | data formatting | bytes 1769472 | tf_op jit(solution)/shard_map/transpose | solution.py:388
  57.7 0.3 copy-done.2
  58.0 0.0 copy-start.1
  58.0 0.5 fusion.7
  58.4 0.2 copy-done.1
  58.7 0.3 reshape.29
  58.9 0.2 reshape.30
  59.2 0.0 copy-start
  59.2 1.8 %fusion.4 = f32[256]{0:T(256)S(1)} fusion(f32[384,256]{1,0:T(8,128)S(1)} %fusion.7, s32[1152]{0:T(1024)S(1)} %get-tuple-element.9, s32[1152]{0:T(1024)S(1)} %get-tuple-element.8, bf16[144,8,2,128]{3,2,1,0:T(2,128)(2,1)S(1)} %bitcast.32), kind=kOutput, calls=%fused_computation.7 | convolution fusion | flops 682868480 | bytes 993280 | tf_op jit(solution)/shard_map/dot_general | solution.py:400
  61.0 0.6 sqrt_bitcast_fusion
  61.6 0.0 copy-done
  61.6 0.3 fusion.14
  61.9 0.6 %reshape.28 = f32[16,2,128]{2,1,0:T(2,128)} reshape(f32[16,256]{1,0:T(8,128)S(1)} %fusion.14) | data formatting | bytes 32768 | tf_op jit(solution)/shard_map/reshape | solution.py:406
  (2 shorter events, 0.0 us)
Async XLA Ops:
  56.9 1.1 %copy-start.2 = (bf16[2,4,16,9,2,128]{5,4,3,2,1,0:T(2,128)(2,1)S(1)}, bf16[2,4,16,9,2,128]{5,4,3,2,1,0:T(2,128)(2,1)}, u32[]{:S(2)}) copy-start(bf16[2,4,16,9,2,128]{5,4,3,2,1,0:T(2,128)(2,1)} %get-tuple-element.7) | copy-start | bytes 1769476
  58.0 0.7 %copy-start.1 = (s32[1152,2]{0,1:T(2,128)S(1)}, s32[1152,2]{0,1:T(2,128)}, u32[]{:S(2)}) copy-start(s32[1152,2]{0,1:T(2,128)} %param.7) | copy-start | bytes 27652
  59.2 2.4 %copy-start = (f32[16,384]{1,0:T(8,128)S(1)}, f32[16,384]{1,0:T(8,128)}, u32[]{:S(2)}) copy-start(f32[16,384]{1,0:T(8,128)} %get-tuple-element.5) | copy-start | bytes 73732

commit v5 on v3

--- a/solution.py
+++ b/solution.py
@@ -144,11 +144,12 @@
     for q in range(last + 1):
         lo, hi = q * LANES, min(q * LANES + LANES, dates)
 
-        @pl.when(tile == q if q < last else tile >= last)
+        @pl.when(tile == q)
         def _(lo=lo, hi=hi):
             piece[:count, : hi - lo] = inverse[:, lo:hi]
 
     column[my_z] = piece[...]
+    pieces = last + 1
 
     counts[...] = reference_counts(region[...], tile, rows, width)
 
@@ -194,8 +195,10 @@
         z_copy(odd * (half - j) + (1 - odd) * (half + j), piece.at[pl.ds(0, even)]).start()
         return carry
 
-    lax.fori_loop(0, nz - 1, send_z, 0)
-    fit[...] = fit_operator(smooth[...], epochs, dates)
+    @pl.when(tile < pieces)
+    def _():
+        lax.fori_loop(0, nz - 1, send_z, 0)
+
 
     for d in range(1, tiles):
         partial_copy(d).wait()
@@ -246,57 +249,76 @@
         device_id=device(my_x, lax.rem(my_z + 1, nz), my_c),
         device_id_type=MESH,
     )
-    arrived.wait()
-    tall = column.shape[1]
-    target = lax.broadcasted_iota(jnp.int32, (nz * count, nz * tall), 0)
-    source = lax.broadcasted_iota(jnp.int32, (nz * count, nz * tall), 1)
-    line = lax.bitwise_and(source, tall - 1)
-    block = lax.shift_right_arithmetic(source, tall.bit_length() - 1)
-    pick = jnp.where((line < count) & (block * count + line == target), 1.0, 0.0)
-    gathered[my_c, tile, my_x] = jnp.dot(
-        pick.astype(jnp.bfloat16),
-        column[...].reshape(nz * tall, LANES),
-        preferred_element_type=jnp.float32,
-    ).astype(jnp.bfloat16)
+    lanes = pl.ds(pl.multiple_of(jnp.minimum(tile, last) * LANES, LANES), LANES)
+
+    @pl.when(tile < pieces)
+    def _():
+        arrived.wait()
+        tall = column.shape[1]
+        target = lax.broadcasted_iota(jnp.int32, (nz * count, nz * tall), 0)
+        source = lax.broadcasted_iota(jnp.int32, (nz * count, nz * tall), 1)
+        line = lax.bitwise_and(source, tall - 1)
+        block = lax.shift_right_arithmetic(source, tall.bit_length() - 1)
+        pick = jnp.where((line < count) & (block * count + line == target), 1.0, 0.0)
+        gathered[my_c, my_x, :, lanes] = jnp.dot(
+            pick.astype(jnp.bfloat16),
+            column[...].reshape(nz * tall, LANES),
+            preferred_element_type=jnp.float32,
+        ).astype(jnp.bfloat16)
+
     second = first + 2 * plane
     lax.fori_loop(first, second, both, 0)
 
     def x_copy(d):
         return pltpu.make_async_remote_copy(
-            src_ref=gathered.at[my_c, tile, my_x],
-            dst_ref=gathered.at[my_c, tile, my_x],
+            src_ref=gathered.at[my_c, my_x, :, lanes],
+            dst_ref=gathered.at[my_c, my_x, :, lanes],
             send_sem=sem.at[base + 2 + 2 * d],
             recv_sem=sem.at[base + 3 + 2 * d],
             device_id=device(lax.rem(my_x + d, nx), my_z, my_c),
             device_id_type=MESH,
         )
 
-    for d in range(1, nx):
-        x_copy(d).start()
+    @pl.when(tile < pieces)
+    def _():
+        for d in range(1, nx):
+            x_copy(d).start()
 
     lax.fori_loop(second, group - 1 - plane, both, 0)
     lax.fori_loop(group - 1 - plane, group - 1, send_block, 0)
+    fit[...] = fit_operator(smooth[...], epochs, dates)
     moved[my_c, my_x, my_z] = corrected(my_x, my_z, my_c)
 
-    for d in range(1, nx):
-        x_copy(d).wait()
+    @pl.when(tile < pieces)
+    def _():
+        for d in range(1, nx):
+            x_copy(d).wait()
 
     over = base + 2 + 2 * nx
 
     def tile_copy(d):
         return pltpu.make_async_remote_copy(
-            src_ref=gathered.at[my_c, tile],
-            dst_ref=gathered.at[my_c, tile],
+            src_ref=gathered.at[my_c, :, :, lanes],
+            dst_ref=gathered.at[my_c, :, :, lanes],
             send_sem=sem.at[over + 2 * d],
             recv_sem=sem.at[over + 1 + 2 * d],
             device_id={"ifg": me, "tile": lax.rem(tile + d, tiles)},
             device_id_type=MESH,
         )
 
+    @pl.when(tile < pieces)
+    def _():
+        for d in range(1, tiles):
+            tile_copy(d).start()
+        for d in range(1, tiles):
+            tile_copy(d).wait_send()
+
     for d in range(1, tiles):
-        tile_copy(d).start()
-    for d in range(1, tiles):
-        tile_copy(d).wait()
+
+        @pl.when(lax.rem(tile + tiles - d, tiles) < pieces)
+        def _(d=d):
+            tile_copy(d).wait_recv()
+
     core = pltpu.make_async_remote_copy(
         src_ref=gathered.at[my_c],
         dst_ref=gathered.at[my_c],
@@ -333,7 +355,7 @@
         functools.partial(exchange, (nx, nz, nc, tiles)),
         out_shape=(
             jax.ShapeDtypeStruct((nc, nx, nz, count, row_count, LANES), jnp.bfloat16),
-            jax.ShapeDtypeStruct((nc, tiles, nx, nz * count, LANES), jnp.bfloat16),
+            jax.ShapeDtypeStruct((nc, nx, nz * count, padded), jnp.bfloat16),
             jax.ShapeDtypeStruct((terms, padded), jnp.float32),
         ),
         in_specs=[pl.BlockSpec(memory_space=pltpu.SMEM)] + [vmem] * 4,
@@ -351,7 +373,7 @@
     )(epochs, ifgs, pseudo_inverse.T, ref_pixels[None, :], smooth)
     total = group * count
     pixel_rows = moved.reshape(total, row_count * LANES)
-    operator = gathered[:, : padded // LANES].transpose(0, 2, 3, 1, 4).reshape(total, padded)
+    operator = gathered.reshape(total, padded)
     displacement = lax.dot_general(
         operator,
         pixel_rows,

time: 61.3 us -> 60 us (0.979)
  local copies, waits for them, and re-layouts: 3.65 us -> 1.15 us
  matrix products: 2.54 us -> 3.89 us
    transpose x2 -> x0, local copies, waits for them, and re-layouts: 1.99 us -> none  [shards(): gathered[:, :padded // LANES].transpose(0, 2, 3, 1, 4)]
    dot_general x1, matrix products: 0.46 us -> 1.81 us  [shards(): lax.dot_general(operator, pixel_rows, (((0,), (0,)), ((), ())), preferred...]
where the time goes in v5:
time: 60 us; the launch traced here: 59.8 us
  Pallas kernels  53.5 us (89%)
  matrix products  3.89 us (6%)
  local copies, waits for them, and re-layouts  1.15 us (2%)
  between operations  0.72 us (1%)
    pallas_call x1, Pallas kernels, shards(): pl.pallas_call(functools.partial(exchange, (nx, nz, nc, tiles)), out_shap...  53.5 us
    dot_general x1, matrix products, shards(): lax.dot_general(operator, pixel_rows, (((0,), (0,)), ((), ())), preferred...  1.81 us
    dot_general x1, matrix products, shards(): jnp.dot(incidence, displacement, precision=lax.Precision.HIGH, preferred_...  1.79 us

profile of v5, /device:TPU:1, one launch (start us, length us, event | category | flops | bytes accessed | tf_op | source)
XLA Modules:
  0.0 59.8 jit_solution(15401489314410855217)
XLA Ops:
  0.6 53.5 %shard_map.77 = (bf16[2,4,16,9,2,128]{5,4,3,2,1,0:T(2,128)(2,1)}, bf16[2,4,144,384]{3,2,1,0:T(8,128)(2,1)}, f32[16,384]{1,0:T(8,128)}) custom-call(s32[8]{0:T(128)} %epochs.1, bf16[9,2,16384]{2,1,0:T(2,128)(2,1)} %ifgs.1, bf16[9,300]{1,0:T(8,128)(2,1)} %bitcast.23, s32[1,64]{1,0:T(1,128)} %bitcast.24, f32[8,384]{1,0:T(8,128)} %constant.9.clone.smooth), custom_call_target="tpu_custom_call" | custom-call | tf_op jit(solution)/shard_map/pallas_call | solution.py:354
  54.1 0.0 copy-start
  54.2 0.0 copy-start.1
  54.2 1.8 %fusion.9 = f32[384,256]{1,0:T(8,128)S(1)} fusion(bf16[1152,384]{1,0:T(8,128)(2,1)} %bitcast.25, bf16[144,8,2,128]{3,2,1,0:T(2,128)(2,1)} %bitcast.26), kind=kOutput, calls=%fused_computation.10 | convolution fusion | flops 226492416 | bytes 1867776 | tf_op jit(solution)/shard_map/dot_general | solution.py:377
  56.0 0.0 copy-done
  56.0 0.0 copy-start.2
  56.0 0.3 fusion.12
  56.3 0.6 %reshape.28 = f32[16,2,128]{2,1,0:T(2,128)} reshape(f32[16,256]{1,0:T(8,128)S(1)} %fusion.12) | data formatting | bytes 32768 | tf_op jit(solution)/shard_map/reshape | solution.py:394
  56.9 0.0 copy-done.1
  56.9 0.3 reshape.29
  57.2 0.2 reshape.30
  57.5 0.0 copy-done.2
  57.5 1.8 %fusion.4 = f32[256]{0:T(256)S(1)} fusion(f32[384,256]{1,0:T(8,128)S(1)} %fusion.9, s32[1152]{0:T(1024)S(1)} %get-tuple-element.9, s32[1152]{0:T(1024)S(1)} %get-tuple-element.8, bf16[144,8,2,128]{3,2,1,0:T(2,128)(2,1)S(1)} %bitcast.27), kind=kOutput, calls=%fused_computation.7 | convolution fusion | flops 682868480 | bytes 993280 | tf_op jit(solution)/shard_map/dot_general | solution.py:388
  59.3 0.6 sqrt_bitcast_fusion
  (2 shorter events, 0.0 us)
Async XLA Ops:
  54.1 1.8 %copy-start = (f32[16,384]{1,0:T(8,128)S(1)}, f32[16,384]{1,0:T(8,128)}, u32[]{:S(2)}) copy-start(f32[16,384]{1,0:T(8,128)} %get-tuple-element.5) | copy-start | bytes 73732
  54.2 2.8 %copy-start.1 = (s32[1152,2]{0,1:T(2,128)S(1)}, s32[1152,2]{0,1:T(2,128)}, u32[]{:S(2)}) copy-start(s32[1152,2]{0,1:T(2,128)} %param.7) | copy-start | bytes 27652
  56.0 1.5 %copy-start.2 = (bf16[2,4,16,9,2,128]{5,4,3,2,1,0:T(2,128)(2,1)S(1)}, bf16[2,4,16,9,2,128]{5,4,3,2,1,0:T(2,128)(2,1)}, u32[]{:S(2)}) copy-start(bf16[2,4,16,9,2,128]{5,4,3,2,1,0:T(2,128)(2,1)} %get-tuple-element.7) | copy-start | bytes 1769476

commit v6 on v5

--- a/solution.py
+++ b/solution.py
@@ -107,11 +107,15 @@
     my_x = lax.div(me, nc * nz)
 
     def place(step):
-        plane = lax.div(step, nx * nc)
-        inner = lax.rem(step, nx * nc)
-        j = lax.div(plane + 1, 2)
-        odd = lax.rem(plane, 2)
-        dz = odd * (half - j) + (1 - odd) * (half + j)
+        side = nx * nc
+        far = 1 - lax.min(lax.div(step, side), 1)
+        later = lax.max(step - side, 0)
+        near = lax.div(later, (nz - 2) * side)
+        j = lax.div(later, 2 * side) + 1
+        within = lax.rem(later, 2 * side)
+        odd = lax.rem(within, 2)
+        inner = far * step + (1 - far) * ((1 - near) * lax.div(within, 2) + near * within)
+        dz = far * half + (1 - far) * (odd * (half - j) + (1 - odd) * (half + j))
         dx = nx - 1 - lax.div(inner, nc)
         dc = nc - 1 - lax.rem(inner, nc)
         return lax.rem(my_x + dx, nx), lax.rem(my_z + dz, nz), lax.rem(my_c + dc, nc)
@@ -354,8 +358,8 @@
     moved, gathered, fit = pl.pallas_call(
         functools.partial(exchange, (nx, nz, nc, tiles)),
         out_shape=(
-            jax.ShapeDtypeStruct((nc, nx, nz, count, row_count, LANES), jnp.bfloat16),
-            jax.ShapeDtypeStruct((nc, nx, nz * count, padded), jnp.bfloat16),
+            pltpu.VMEM((nc, nx, nz, count, row_count, LANES), jnp.bfloat16),
+            pltpu.VMEM((nc, nx, nz * count, padded), jnp.bfloat16),
             jax.ShapeDtypeStruct((terms, padded), jnp.float32),
         ),
         in_specs=[pl.BlockSpec(memory_space=pltpu.SMEM)] + [vmem] * 4,

time: 60 us -> 59 us (0.983)
  matrix products: 3.89 us -> 2.55 us
    dot_general x1, matrix products: 1.81 us -> 0.47 us  [shards(): lax.dot_general(operator, pixel_rows, (((0,), (0,)), ((), ())), preferred...]
where the time goes in v6:
time: 59 us; the launch traced here: 58.8 us
  Pallas kernels  53.6 us (91%)
  matrix products  2.55 us (4%)
  local copies, waits for them, and re-layouts  1.37 us (2%)
  between operations  0.69 us (1%)
    pallas_call x1, Pallas kernels, shards(): pl.pallas_call(functools.partial(exchange, (nx, nz, nc, tiles)), out_shap...  53.6 us
    dot_general x1, matrix products, shards(): jnp.dot(incidence, displacement, precision=lax.Precision.HIGH, preferred_...  1.79 us

profile of v6, /device:TPU:1, one launch (start us, length us, event | category | flops | bytes accessed | tf_op | source)
XLA Modules:
  0.0 58.8 jit_solution(5497762705176002823)
XLA Ops:
  0.6 53.6 %shard_map.77 = (bf16[2,4,16,9,2,128]{5,4,3,2,1,0:T(2,128)(2,1)S(1)}, bf16[2,4,144,384]{3,2,1,0:T(8,128)(2,1)S(1)}, f32[16,384]{1,0:T(8,128)}) custom-call(s32[8]{0:T(128)} %epochs.1, bf16[9,2,16384]{2,1,0:T(2,128)(2,1)} %ifgs.1, bf16[9,300]{1,0:T(8,128)(2,1)} %bitcast.26, s32[1,64]{1,0:T(1,128)} %bitcast.27, f32[8,384]{1,0:T(8,128)} %constant.9.clone.smooth), custom_call_target="tpu_custom_call" | custom-call | tf_op jit(solution)/shard_map/pallas_call | solution.py:358
  54.2 0.0 copy-start
  54.3 0.0 copy-start.1
  54.3 0.5 fusion.9
  54.7 0.2 copy-done
  55.0 0.3 fusion.12
  55.3 0.6 %reshape.28 = f32[16,2,128]{2,1,0:T(2,128)} reshape(f32[16,256]{1,0:T(8,128)S(1)} %fusion.12) | data formatting | bytes 32768 | tf_op jit(solution)/shard_map/reshape | solution.py:398
  55.9 0.0 copy-done.1
  55.9 0.3 reshape.29
  56.2 0.2 reshape.30
  56.4 1.8 %fusion.4 = f32[256]{0:T(256)S(1)} fusion(f32[384,256]{1,0:T(8,128)S(1)} %fusion.9, s32[1152]{0:T(1024)S(1)} %get-tuple-element.9, s32[1152]{0:T(1024)S(1)} %get-tuple-element.8, bf16[144,8,2,128]{3,2,1,0:T(2,128)(2,1)S(1)} %bitcast.24), kind=kOutput, calls=%fused_computation.7 | convolution fusion | flops 682868480 | bytes 993280 | tf_op jit(solution)/shard_map/dot_general | solution.py:392
  58.2 0.6 sqrt_bitcast_fusion
  (2 shorter events, 0.0 us)
Async XLA Ops:
  54.2 0.7 %copy-start = (f32[16,384]{1,0:T(8,128)S(1)}, f32[16,384]{1,0:T(8,128)}, u32[]{:S(2)}) copy-start(f32[16,384]{1,0:T(8,128)} %get-tuple-element.5) | copy-start | bytes 73732
  54.3 1.7 %copy-start.1 = (s32[1152,2]{0,1:T(2,128)S(1)}, s32[1152,2]{0,1:T(2,128)}, u32[]{:S(2)}) copy-start(s32[1152,2]{0,1:T(2,128)} %param.7) | copy-start | bytes 27652

commit v7 on v6

--- a/solution.py
+++ b/solution.py
@@ -32,12 +32,12 @@
 
 
 def fit_operator(smooth, epochs, count):
-    steps = epochs.shape[0]
+    steps = epochs.shape[1]
     index = lax.broadcasted_iota(jnp.int32, (steps, smooth.shape[1]), 1)
     which = lax.broadcasted_iota(jnp.int32, (steps, smooth.shape[1]), 0)
     start = jnp.zeros_like(index)
     for e in range(steps):
-        start = jnp.where(which == e, epochs[e], start)
+        start = jnp.where(which == e, epochs[:, e : e + 1], start)
     jumps = jnp.where((index >= start) & (index < count), 1.0, 0.0)
     right = jnp.concatenate([smooth, jumps], axis=0)
     terms = right.shape[0]
@@ -93,10 +93,14 @@
 
 
 def exchange(
-    dims, epochs, ifgs, inverse, region, smooth,
-    moved, gathered, fit,
+    dims, *refs,
+):
+    far_refs, (moved, gathered, fit), rest = refs[:5], refs[5:8], refs[8:]
+    near_refs = rest[:5]
+    epochs, ifgs, inverse, region, smooth = near_refs
+    (
     sent, piece, column, counts, local, sums, sem,
-):
+    ) = rest[5:]
     nx, nz, nc, tiles = dims
     group = nx * nz * nc
     half = nz // 2
@@ -123,6 +127,13 @@
     def device(x, z, c):
         return {"ifg": (x * nz + z) * nc + c, "tile": tile}
 
+    last_sem = sem.shape[0] - 5
+    loads = [
+        pltpu.make_async_copy(source, target, sem.at[last_sem + i])
+        for i, (source, target) in enumerate(zip(far_refs, near_refs))
+    ]
+    for load in loads:
+        load.start()
     column[...] = jnp.zeros_like(column)
     barrier = pltpu.get_barrier_semaphore()
 
@@ -143,6 +154,8 @@
 
     count, rows, width = ifgs.shape
     dates = inverse.shape[1]
+    for load in loads:
+        load.wait()
     piece[...] = jnp.zeros_like(piece)
     last = -(-dates // LANES) - 1
     for q in range(last + 1):
@@ -290,7 +303,7 @@
 
     lax.fori_loop(second, group - 1 - plane, both, 0)
     lax.fori_loop(group - 1 - plane, group - 1, send_block, 0)
-    fit[...] = fit_operator(smooth[...], epochs, dates)
+    fit[...] = fit_operator(smooth[...], epochs[...], dates)
     moved[my_c, my_x, my_z] = corrected(my_x, my_z, my_c)
 
     @pl.when(tile < pieces)
@@ -355,26 +368,28 @@
     vmem = pl.BlockSpec(memory_space=pltpu.VMEM)
     smooth = jnp.asarray(smooth_columns(date_count, padded))
     terms = smooth.shape[0] + epochs.shape[0]
+    operands = (epochs[None, :], ifgs, pseudo_inverse.T, ref_pixels[None, :], smooth)
     moved, gathered, fit = pl.pallas_call(
         functools.partial(exchange, (nx, nz, nc, tiles)),
         out_shape=(
             pltpu.VMEM((nc, nx, nz, count, row_count, LANES), jnp.bfloat16),
             pltpu.VMEM((nc, nx, nz * count, padded), jnp.bfloat16),
-            jax.ShapeDtypeStruct((terms, padded), jnp.float32),
+            pltpu.VMEM((terms, padded), jnp.float32),
         ),
-        in_specs=[pl.BlockSpec(memory_space=pltpu.SMEM)] + [vmem] * 4,
+        in_specs=[pl.BlockSpec(memory_space=pltpu.HBM)] * 5,
         out_specs=(vmem,) * 3,
-        scratch_shapes=[
+        scratch_shapes=[pltpu.VMEM(a.shape, a.dtype) for a in operands]
+        + [
             pltpu.VMEM((group, count, row_count, LANES), jnp.bfloat16),
             pltpu.VMEM((tall, LANES), jnp.bfloat16),
             pltpu.VMEM((nz, tall, LANES), jnp.bfloat16),
             pltpu.VMEM((col_total // LANES * row_count, LANES), jnp.float32),
             pltpu.VMEM((count, row_count, LANES), jnp.float32),
             pltpu.VMEM((tiles - 1, count, row_count, LANES), jnp.float32),
-            pltpu.SemaphoreType.DMA((4 * tiles + 2 * nx + 4,)),
+            pltpu.SemaphoreType.DMA((4 * tiles + 2 * nx + 9,)),
         ],
         compiler_params=pltpu.CompilerParams(collective_id=0, has_side_effects=True),
-    )(epochs, ifgs, pseudo_inverse.T, ref_pixels[None, :], smooth)
+    )(*operands)
     total = group * count
     pixel_rows = moved.reshape(total, row_count * LANES)
     operator = gathered.reshape(total, padded)

time: 59 us -> 57 us (0.966)
  Pallas kernels: 53.6 us -> 52 us
    pallas_call x1, Pallas kernels: 53.6 us -> 52 us  [shards(): pl.pallas_call(functools.partial(exchange, (nx, nz, nc, tiles)), out_shap...]
where the time goes in v7:
time: 57 us; the launch traced here: 56.9 us
  Pallas kernels  52 us (91%)
  matrix products  2.56 us (4%)
  local copies, waits for them, and re-layouts  1.14 us (2%)
  between operations  0.68 us (1%)
  other arithmetic  0.58 us (1%)
    pallas_call x1, Pallas kernels, shards(): pl.pallas_call(functools.partial(exchange, (nx, nz, nc, tiles)), out_shap...  52 us
    dot_general x1, matrix products, shards(): jnp.dot(incidence, displacement, precision=lax.Precision.HIGH, preferred_...  1.79 us

profile of v7, /device:TPU:1, one launch (start us, length us, event | category | flops | bytes accessed | tf_op | source)
XLA Modules:
  0.0 56.9 jit_solution(13022208309091744793)
XLA Ops:
  0.6 52.0 %shard_map.77 = (bf16[2,4,16,9,2,128]{5,4,3,2,1,0:T(2,128)(2,1)S(1)}, bf16[2,4,144,384]{3,2,1,0:T(8,128)(2,1)S(1)}, f32[16,384]{1,0:T(8,128)S(1)}) custom-call(s32[1,8]{1,0:T(1,128)} %bitcast.28, bf16[9,2,16384]{2,1,0:T(2,128)(2,1)} %refs_1_.1, bf16[9,300]{1,0:T(8,128)(2,1)} %bitcast.27, s32[1,64]{1,0:T(1,128)} %bitcast.29, f32[8,384]{1,0:T(8,128)} %constant.9.clone.refs_4_), custom_call_target="tpu_custom_call" | custom-call | tf_op jit(solution)/shard_map/pallas_call | solution.py:372
  52.6 0.0 copy-start
  52.6 0.5 fusion.9
  53.1 0.3 fusion.12
  53.4 0.6 %reshape.28 = f32[16,2,128]{2,1,0:T(2,128)} reshape(f32[16,256]{1,0:T(8,128)S(1)} %fusion.12) | data formatting | bytes 32768 | tf_op jit(solution)/shard_map/reshape | solution.py:413
  54.0 0.0 copy-done
  54.0 0.3 reshape.29
  54.3 0.2 reshape.30
  54.6 1.8 %fusion.4 = f32[256]{0:T(256)S(1)} fusion(f32[384,256]{1,0:T(8,128)S(1)} %fusion.9, s32[1152]{0:T(1024)S(1)} %get-tuple-element.9, s32[1152]{0:T(1024)S(1)} %get-tuple-element.8, bf16[144,8,2,128]{3,2,1,0:T(2,128)(2,1)S(1)} %bitcast.25), kind=kOutput, calls=%fused_computation.7 | convolution fusion | flops 682868480 | bytes 993280 | tf_op jit(solution)/shard_map/dot_general | solution.py:407
  56.3 0.6 %sqrt_bitcast_fusion = f32[2,128]{1,0:T(2,128)} fusion(f32[256]{0:T(256)S(1)} %fusion.4), kind=kLoop, calls=%fused_computation.15 | loop fusion | flops 512 | bytes 2048 | tf_op jit(solution)/shard_map/sqrt | solution.py:411
  (2 shorter events, 0.0 us)
Async XLA Ops:
  52.6 1.4 %copy-start = (s32[1152,2]{0,1:T(2,128)S(1)}, s32[1152,2]{0,1:T(2,128)}, u32[]{:S(2)}) copy-start(s32[1152,2]{0,1:T(2,128)} %param.7) | copy-start | bytes 27652

commit v8 on v7

--- a/solution.py
+++ b/solution.py
@@ -138,12 +138,11 @@
     barrier = pltpu.get_barrier_semaphore()
 
     def greet(step, carry):
-        pl.semaphore_signal(
-            barrier, inc=1, device_id=device(*place(step)), device_id_type=MESH
-        )
+        peer = {"ifg": lax.rem(me + step, group), "tile": tile}
+        pl.semaphore_signal(barrier, inc=1, device_id=peer, device_id_type=MESH)
         return carry
 
-    lax.fori_loop(0, group - 1, greet, 0)
+    lax.fori_loop(1, group, greet, 0)
     for d in range(1, tiles):
         pl.semaphore_signal(
             barrier,

time: 57 us -> 57.2 us (level)
  no operation moved by 1% of the time
where the time goes in v8:
time: 57.2 us; the launch traced here: 57.1 us
  Pallas kernels  52.2 us (91%)
  matrix products  2.56 us (4%)
  local copies, waits for them, and re-layouts  1.14 us (2%)
  between operations  0.69 us (1%)
  other arithmetic  0.58 us (1%)
    pallas_call x1, Pallas kernels, shards(): pl.pallas_call(functools.partial(exchange, (nx, nz, nc, tiles)), out_shap...  52.2 us
    dot_general x1, matrix products, shards(): jnp.dot(incidence, displacement, precision=lax.Precision.HIGH, preferred_...  1.79 us

profile of v8, /device:TPU:1, one launch (start us, length us, event | category | flops | bytes accessed | tf_op | source)
XLA Modules:
  0.0 57.1 jit_solution(18224068251947344911)
XLA Ops:
  0.6 52.2 %shard_map.77 = (bf16[2,4,16,9,2,128]{5,4,3,2,1,0:T(2,128)(2,1)S(1)}, bf16[2,4,144,384]{3,2,1,0:T(8,128)(2,1)S(1)}, f32[16,384]{1,0:T(8,128)S(1)}) custom-call(s32[1,8]{1,0:T(1,128)} %bitcast.28, bf16[9,2,16384]{2,1,0:T(2,128)(2,1)} %refs_1_.1, bf16[9,300]{1,0:T(8,128)(2,1)} %bitcast.27, s32[1,64]{1,0:T(1,128)} %bitcast.29, f32[8,384]{1,0:T(8,128)} %constant.9.clone.refs_4_), custom_call_target="tpu_custom_call" | custom-call | tf_op jit(solution)/shard_map/pallas_call | solution.py:371
  52.8 0.0 copy-start
  52.8 0.5 fusion.9
  53.3 0.3 fusion.12
  53.6 0.6 %reshape.28 = f32[16,2,128]{2,1,0:T(2,128)} reshape(f32[16,256]{1,0:T(8,128)S(1)} %fusion.12) | data formatting | bytes 32768 | tf_op jit(solution)/shard_map/reshape | solution.py:412
  54.2 0.0 copy-done
  54.2 0.3 reshape.29
  54.5 0.2 reshape.30
  54.8 1.8 %fusion.4 = f32[256]{0:T(256)S(1)} fusion(f32[384,256]{1,0:T(8,128)S(1)} %fusion.9, s32[1152]{0:T(1024)S(1)} %get-tuple-element.9, s32[1152]{0:T(1024)S(1)} %get-tuple-element.8, bf16[144,8,2,128]{3,2,1,0:T(2,128)(2,1)S(1)} %bitcast.25), kind=kOutput, calls=%fused_computation.7 | convolution fusion | flops 682868480 | bytes 993280 | tf_op jit(solution)/shard_map/dot_general | solution.py:406
  56.6 0.6 %sqrt_bitcast_fusion = f32[2,128]{1,0:T(2,128)} fusion(f32[256]{0:T(256)S(1)} %fusion.4), kind=kLoop, calls=%fused_computation.15 | loop fusion | flops 512 | bytes 2048 | tf_op jit(solution)/shard_map/sqrt | solution.py:410
  (2 shorter events, 0.0 us)
Async XLA Ops:
  52.8 1.4 %copy-start = (s32[1152,2]{0,1:T(2,128)S(1)}, s32[1152,2]{0,1:T(2,128)}, u32[]{:S(2)}) copy-start(s32[1152,2]{0,1:T(2,128)} %param.7) | copy-start | bytes 27652
